TPU v7x, 256 devices: a whole 4x4x8 slice. The times are simulated.
256 devices in a mesh: dp: 8 (over z), seq: 32 (over x, y, core).
Axes of the slice: x: 4, y: 4, z: 8, core: 2. Of those that a mesh axis runs over, the one named last changes fastest.
Arguments:
- hidden: bfloat16 [32768, 5120], P(('dp', 'seq')), may hold values from -24 to 24
- queries: bfloat16 [32768, 4096], P(('dp', 'seq')), may hold values from -330 to 330
- key_states: bfloat16 [32768, 4096], P(('dp', 'seq')), may hold values from -18 to 18
- value_states: bfloat16 [32768, 4096], P(('dp', 'seq')), may hold values from -6 to 6
- attention_out: bfloat16 [32768, 4096], P(('dp', 'seq')), may hold values from -6 to 6
- grad_out: bfloat16 [32768, 4096], P(('dp', 'seq')), may hold values from -24 to 24
- lengths: int32 [8, 4], P('dp'), may hold values from 1 to 2048, 4096 in all within a row
- down_query: bfloat16 [8, 5120], replicated, may hold values from -0.00048828125 to 0.00048828125
- up_query: bfloat16 [8, 4096], replicated, may hold values from -0.00048828125 to 0.00048828125
- down_value: bfloat16 [8, 5120], replicated, may hold values from -0.00048828125 to 0.00048828125
- up_value: bfloat16 [8, 4096], replicated, may hold values from -0.00048828125 to 0.00048828125
Outputs:
- grad_queries: bfloat16 [32768, 4096], P(('dp', 'seq'))
- grad_keys: bfloat16 [32768, 4096], P(('dp', 'seq'))
- value_gradients: bfloat16 [32768, 4096], P(('dp', 'seq'))
- query_down_gradient: float32 [8, 5120], P(None, 'dp')
- query_up_gradient: float32 [8, 4096], P(None, 'dp')
- value_down_gradient: float32 [8, 5120], P(None, 'dp')
- value_up_gradient: float32 [8, 4096], P(None, 'dp')
Inputs may be any that keep to these rules, and one draw needn't show every extreme that they name: Each row lists the lengths of the 4 sequences of one pack in packing order; a row sums to 4096.
All inputs are finite; a program needn't handle non-finite values.
Results may differ from a plain program's by a relative error of at most 0.0067.
Values may be sent and summed in bfloat16 or wider, within the bound.
A program may use at most 64 MiB of HBM per device.

v0:
```python
import math

import jax
import jax.numpy as jnp
from jax import lax
from jax.sharding import PartitionSpec as P

H = 32
HD = 128
ADAPTER_RANK = 8
ADAPTER_ALPHA = 16


def pack_begin(lengths_row, total):
    seq_ends = jnp.cumsum(lengths_row)
    starts = seq_ends - lengths_row
    positions = jnp.arange(total, dtype=jnp.int32)
    inside = (positions[:, None] >= starts[None, :]) & (positions[:, None] < seq_ends[None, :])
    return jnp.sum(jnp.where(inside, starts[None, :], 0), axis=1)


def rotate_back(grads, seq_positions):
    rows = grads.shape[0]
    half = HD // 2
    inverse = jnp.exp(-(jnp.arange(half, dtype=jnp.float32) * (2.0 / HD)) * math.log(10000.0))
    angles = seq_positions.astype(jnp.float32)[:, None] * inverse[None, :]
    cosine = jnp.cos(angles)[:, None, :]
    sine = jnp.sin(angles)[:, None, :]
    split = grads.astype(jnp.float32).reshape(rows, H, HD)
    first = split[:, :, :half]
    second = split[:, :, half:]
    new_first = first * cosine + second * sine
    new_second = second * cosine - first * sine
    joined = jnp.concatenate([new_first, new_second], axis=2)
    return joined.reshape(rows, H * HD).astype(jnp.bfloat16)


def head_backward(head_query, head_key, head_value, head_grad, delta_column, begin, block_rows):
    total = head_query.shape[0]
    width = head_query.shape[1]
    block_count = total // block_rows
    scaling = 1.0 / math.sqrt(width)
    offsets = jnp.arange(block_rows, dtype=jnp.int32)

    def block_of(array, index):
        return lax.dynamic_slice_in_dim(array, index * block_rows, block_rows, 0)

    def outer(query_block, running):
        grad_query_all, grad_key_all, grad_value_all = running
        query_rows = block_of(head_query, query_block)
        grad_rows = block_of(head_grad, query_block)
        delta_rows = block_of(delta_column, query_block)[:, None]
        row_begin = block_of(begin, query_block)
        row_positions = query_block * block_rows + offsets
        first_block = row_begin[0] // block_rows

        def allowed_at(key_block):
            key_positions = key_block * block_rows + offsets
            return (key_positions[None, :] >= row_begin[:, None]) & (
                key_positions[None, :] <= row_positions[:, None]
            )

        def scores_at(key_block):
            key_rows = block_of(head_key, key_block)
            return jnp.dot(query_rows, key_rows.T, preferred_element_type=jnp.float32) * scaling

        def statistics(key_block, running_stats):
            row_top, row_total = running_stats
            allowed = allowed_at(key_block)
            masked = jnp.where(allowed, scores_at(key_block), -1e30)
            new_top = jnp.maximum(row_top, jnp.max(masked, axis=1, keepdims=True))
            weights = jnp.where(allowed, jnp.exp(masked - new_top), 0.0)
            row_total = row_total * jnp.exp(row_top - new_top) + jnp.sum(
                weights, axis=1, keepdims=True
            )
            return (new_top, row_total)

        start_stats = (
            jnp.full((block_rows, 1), -1e30, jnp.float32),
            jnp.zeros((block_rows, 1), jnp.float32),
        )
        row_top, row_total = lax.fori_loop(first_block, query_block + 1, statistics, start_stats)

        def gradients(key_block, running_grads):
            grad_query_rows, grad_key_acc, grad_value_acc = running_grads
            key_rows = block_of(head_key, key_block)
            value_rows = block_of(head_value, key_block)
            allowed = allowed_at(key_block)
            prob_rows = jnp.where(allowed, jnp.exp(scores_at(key_block) - row_top) / row_total, 0.0)
            prob_low = prob_rows.astype(jnp.bfloat16)
            grad_prob = jnp.dot(grad_rows, value_rows.T, preferred_element_type=jnp.float32)
            grad_score = (prob_rows * (grad_prob - delta_rows)).astype(jnp.bfloat16)
            grad_query_rows = grad_query_rows + jnp.dot(
                grad_score, key_rows, preferred_element_type=jnp.float32
            )
            key_piece = jnp.dot(grad_score.T, query_rows, preferred_element_type=jnp.float32)
            value_piece = jnp.dot(prob_low.T, grad_rows, preferred_element_type=jnp.float32)
            grad_key_acc = lax.dynamic_update_slice_in_dim(
                grad_key_acc,
                block_of(grad_key_acc, key_block) + key_piece,
                key_block * block_rows,
                0,
            )
            grad_value_acc = lax.dynamic_update_slice_in_dim(
                grad_value_acc,
                block_of(grad_value_acc, key_block) + value_piece,
                key_block * block_rows,
                0,
            )
            return (grad_query_rows, grad_key_acc, grad_value_acc)

        start_grads = (jnp.zeros((block_rows, width), jnp.float32), grad_key_all, grad_value_all)
        grad_query_rows, grad_key_all, grad_value_all = lax.fori_loop(
            first_block, query_block + 1, gradients, start_grads
        )
        grad_query_all = lax.dynamic_update_slice_in_dim(
            grad_query_all, grad_query_rows * scaling, query_block * block_rows, 0
        )
        return (grad_query_all, grad_key_all, grad_value_all)

    empty_rows = jnp.zeros((total, width), jnp.float32)
    grad_query_all, grad_key_all, grad_value_all = lax.fori_loop(
        0, block_count, outer, (empty_rows, empty_rows, empty_rows)
    )
    return (
        grad_query_all.astype(jnp.bfloat16),
        (grad_key_all * scaling).astype(jnp.bfloat16),
        grad_value_all.astype(jnp.bfloat16),
    )


def shards(
    hidden,
    queries,
    key_states,
    value_states,
    attention_out,
    grad_out,
    lengths,
    down_query,
    up_query,
    down_value,
    up_value,
):
    tok_rows = queries.shape[0]
    members = lax.axis_size("seq")
    total = tok_rows * members
    heads_here = H // members
    block_rows = min(512, total)
    begin = pack_begin(lengths[0], total)
    head_query, head_key, head_value, head_out, head_grad = (
        lax.all_to_all(queries, "seq", split_axis=1, concat_axis=0, tiled=True),
        lax.all_to_all(key_states, "seq", split_axis=1, concat_axis=0, tiled=True),
        lax.all_to_all(value_states, "seq", split_axis=1, concat_axis=0, tiled=True),
        lax.all_to_all(attention_out, "seq", split_axis=1, concat_axis=0, tiled=True),
        lax.all_to_all(grad_out, "seq", split_axis=1, concat_axis=0, tiled=True),
    )
    products = head_out.astype(jnp.float32) * head_grad.astype(jnp.float32)
    row_delta = jnp.sum(products.reshape(total, heads_here, HD), axis=2)
    grad_query, grad_key, grad_value = head_backward(
        head_query, head_key, head_value, head_grad, row_delta[:, 0], begin, block_rows
    )
    grad_queries, grad_keys, value_gradients = (
        lax.all_to_all(grad_query, "seq", split_axis=0, concat_axis=1, tiled=True),
        lax.all_to_all(grad_key, "seq", split_axis=0, concat_axis=1, tiled=True),
        lax.all_to_all(grad_value, "seq", split_axis=0, concat_axis=1, tiled=True),
    )
    first_row = lax.axis_index("seq") * tok_rows
    local_begin = lax.dynamic_slice_in_dim(begin, first_row, tok_rows, 0)
    seq_positions = first_row + jnp.arange(tok_rows, dtype=jnp.int32) - local_begin
    query_gradient_before = rotate_back(grad_queries, seq_positions)
    query_lowrank = jnp.dot(hidden, down_query.T, preferred_element_type=jnp.float32).astype(
        jnp.bfloat16
    )
    value_lowrank = jnp.dot(hidden, down_value.T, preferred_element_type=jnp.float32).astype(
        jnp.bfloat16
    )
    query_backprop = jnp.dot(
        query_gradient_before, up_query.T, preferred_element_type=jnp.float32
    ).astype(jnp.bfloat16)
    value_backprop = jnp.dot(
        value_gradients, up_value.T, preferred_element_type=jnp.float32
    ).astype(jnp.bfloat16)
    terms = (
        jnp.dot(query_backprop.T, hidden, preferred_element_type=jnp.float32),
        jnp.dot(query_lowrank.T, query_gradient_before, preferred_element_type=jnp.float32),
        jnp.dot(value_backprop.T, hidden, preferred_element_type=jnp.float32),
        jnp.dot(value_lowrank.T, value_gradients, preferred_element_type=jnp.float32),
    )
    summed = lax.psum((terms[0], terms[1], terms[2], terms[3]), "seq")
    group_portions = (
        lax.psum_scatter(summed[0], "dp", scatter_dimension=1, tiled=True),
        lax.psum_scatter(summed[1], "dp", scatter_dimension=1, tiled=True),
        lax.psum_scatter(summed[2], "dp", scatter_dimension=1, tiled=True),
        lax.psum_scatter(summed[3], "dp", scatter_dimension=1, tiled=True),
    )
    adapter_scale = ADAPTER_ALPHA / ADAPTER_RANK
    return (
        grad_queries,
        grad_keys,
        value_gradients,
        group_portions[0] * adapter_scale,
        group_portions[1] * adapter_scale,
        group_portions[2] * adapter_scale,
        group_portions[3] * adapter_scale,
    )


def solution(mesh):
    placed = (
        P(("dp", "seq"), None),
        P(("dp", "seq"), None),
        P(("dp", "seq"), None),
        P(("dp", "seq"), None),
        P(("dp", "seq"), None),
        P(("dp", "seq"), None),
        P("dp", None),
        P(),
        P(),
        P(),
        P(),
    )
    return jax.shard_map(
        shards,
        mesh=mesh,
        in_specs=placed,
        out_specs=(
            P(("dp", "seq"), None),
            P(("dp", "seq"), None),
            P(("dp", "seq"), None),
            P(None, "dp"),
            P(None, "dp"),
            P(None, "dp"),
            P(None, "dp"),
        ),
        check_vma=False,
    )
```

profile of v0, /device:TPU:1, one launch (start us, length us, event | category | flops | bytes accessed | tf_op | source)
XLA Modules:
  0.0 631.5 jit_solution(7207418629634255673)
XLA Ops:
  7.2 2.6 copy_bitcast_fusion.4
  9.8 8.6 %all-to-all-start = ((bf16[128,32,128]{2,0,1:T(8,128)(2,1)}), bf16[128,32,128]{2,0,1:T(8,128)(2,1)S(1)}, u32[]{:S(2)}, u32[]{:S(2)}) async-start(bf16[128,32,128]{2,0,1:T(8,128)(2,1)} %copy_bitcast_fusion.4), calls=%async_computation | async-start | bytes 2097152 | tf_op jit(solution)/shard_map/all_to_all | solution.py:152
  19.7 15.6 %all-to-all-done = bf16[128,32,128]{2,0,1:T(8,128)(2,1)S(1)} async-done(((bf16[128,32,128]{2,0,1:T(8,128)(2,1)}), bf16[128,32,128]{2,0,1:T(8,128)(2,1)S(1)}, u32[]{:S(2)}, u32[]{:S(2)}) %all-to-all-start) | async-done | bytes 1048608 | tf_op jit(solution)/shard_map/all_to_all | solution.py:152
  36.3 4.0 all-to-all-start.1
  40.3 2.5 copy_bitcast_fusion.2
  42.8 14.4 %all-to-all-done.1 = bf16[128,32,128]{2,0,1:T(8,128)(2,1)S(1)} async-done(((bf16[128,32,128]{2,0,1:T(8,128)(2,1)}), bf16[128,32,128]{2,0,1:T(8,128)(2,1)S(1)}, u32[]{:S(2)}, u32[]{:S(2)}) %all-to-all-start.1) | async-done | bytes 1048608 | tf_op jit(solution)/shard_map/all_to_all | solution.py:153
  57.2 4.5 all-to-all-start.2
  61.7 2.5 copy_bitcast_fusion.1
  64.1 14.5 %all-to-all-done.2 = bf16[128,32,128]{2,0,1:T(8,128)(2,1)} async-done(((bf16[128,32,128]{2,0,1:T(8,128)(2,1)}), bf16[128,32,128]{2,0,1:T(8,128)(2,1)}, u32[]{:S(2)}, u32[]{:S(2)}) %all-to-all-start.2) | async-done | bytes 1048608 | tf_op jit(solution)/shard_map/all_to_all | solution.py:156
  78.6 4.4 all-to-all-start.3
  83.3 2.5 copy_bitcast_fusion
  85.7 14.3 %all-to-all-done.3 = bf16[128,32,128]{2,0,1:T(8,128)(2,1)} async-done(((bf16[128,32,128]{2,0,1:T(8,128)(2,1)}), bf16[128,32,128]{2,0,1:T(8,128)(2,1)}, u32[]{:S(2)}, u32[]{:S(2)}) %all-to-all-start.3) | async-done | bytes 1048608 | tf_op jit(solution)/shard_map/all_to_all | solution.py:155
  100.1 4.5 all-to-all-start.4
  105.7 2.2 fusion.23
  107.8 13.7 %all-to-all-done.4 = bf16[128,32,128]{2,0,1:T(8,128)(2,1)} async-done(((bf16[128,32,128]{2,0,1:T(8,128)(2,1)}), bf16[128,32,128]{2,0,1:T(8,128)(2,1)}, u32[]{:S(2)}, u32[]{:S(2)}) %all-to-all-start.4) | async-done | bytes 1048608 | tf_op jit(solution)/shard_map/all_to_all | solution.py:154
  124.4 182.3 %while.106 = (s32[]{:T(128)}, bf16[4096,128]{1,0:T(8,128)(2,1)}, f32[4096,128]{1,0:T(8,128)}, f32[4096,128]{1,0:T(8,128)}, s32[4096]{0:T(1024)S(1)}, /*index=5*/...) while((s32[]{:T(128)}, bf16[4096,128]{1,0:T(8,128)(2,1)}, ...), condition=%wide.region_10.11_spmd.clone.clone, body=%wide.region_3.10_spmd.clone.clone.sunk | while | flops 408947232 | bytes 10955935 | solution.py:122
  129.5 6.0 while.108
  142.1 12.0 %while.108 = (s32[]{:T(128)}, f32[512,128]{1,0:T(8,128)S(1)}, f32[4096,128]{1,0:T(8,128)}, f32[4096,128]{1,0:T(8,128)}, s32[]{:T(128)}, /*index=5*/s32[512]{0:T(...) while((s32[]{:T(128)}, f32[512,128]{1,0:T(8,128)S(1)}, ...), condition=%wide.region_9.9_spmd, body=%wide.region_8.8_spmd.sunk | while | flops 338625024 | bytes 7225595 | solution.py:113
  160.7 12.0 %while.108 = (s32[]{:T(128)}, f32[512,128]{1,0:T(8,128)S(1)}, f32[4096,128]{1,0:T(8,128)}, f32[4096,128]{1,0:T(8,128)}, s32[]{:T(128)}, /*index=5*/s32[512]{0:T(...) while((s32[]{:T(128)}, f32[512,128]{1,0:T(8,128)S(1)}, ...), condition=%wide.region_9.9_spmd, body=%wide.region_8.8_spmd.sunk | while | flops 338625024 | bytes 7225595 | solution.py:113
  170.7 2.0 fusion.86
  177.6 2.4 while.107
  180.1 18.0 %while.108 = (s32[]{:T(128)}, f32[512,128]{1,0:T(8,128)S(1)}, f32[4096,128]{1,0:T(8,128)}, f32[4096,128]{1,0:T(8,128)}, s32[]{:T(128)}, /*index=5*/s32[512]{0:T(...) while((s32[]{:T(128)}, f32[512,128]{1,0:T(8,128)S(1)}, ...), condition=%wide.region_9.9_spmd, body=%wide.region_8.8_spmd.sunk | while | flops 338625024 | bytes 7225595 | solution.py:113
  190.1 2.0 fusion.86
  194.1 2.0 fusion.85
  196.1 2.0 fusion.86
  202.9 3.1 while.107
  206.2 23.9 %while.108 = (s32[]{:T(128)}, f32[512,128]{1,0:T(8,128)S(1)}, f32[4096,128]{1,0:T(8,128)}, f32[4096,128]{1,0:T(8,128)}, s32[]{:T(128)}, /*index=5*/s32[512]{0:T(...) while((s32[]{:T(128)}, f32[512,128]{1,0:T(8,128)S(1)}, ...), condition=%wide.region_9.9_spmd, body=%wide.region_8.8_spmd.sunk | while | flops 338625024 | bytes 7225595 | solution.py:113
  216.2 2.0 fusion.86
  222.2 2.0 fusion.86
  235.0 3.9 while.107
  239.1 29.9 %while.108 = (s32[]{:T(128)}, f32[512,128]{1,0:T(8,128)S(1)}, f32[4096,128]{1,0:T(8,128)}, f32[4096,128]{1,0:T(8,128)}, s32[]{:T(128)}, /*index=5*/s32[512]{0:T(...) while((s32[]{:T(128)}, f32[512,128]{1,0:T(8,128)S(1)}, ...), condition=%wide.region_9.9_spmd, body=%wide.region_8.8_spmd.sunk | while | flops 338625024 | bytes 7225595 | solution.py:113
  249.1 2.0 fusion.86
  255.1 2.0 fusion.86
  275.5 11.9 %while.108 = (s32[]{:T(128)}, f32[512,128]{1,0:T(8,128)S(1)}, f32[4096,128]{1,0:T(8,128)}, f32[4096,128]{1,0:T(8,128)}, s32[]{:T(128)}, /*index=5*/s32[512]{0:T(...) while((s32[]{:T(128)}, f32[512,128]{1,0:T(8,128)S(1)}, ...), condition=%wide.region_9.9_spmd, body=%wide.region_8.8_spmd.sunk | while | flops 338625024 | bytes 7225595 | solution.py:113
  294.1 11.9 %while.108 = (s32[]{:T(128)}, f32[512,128]{1,0:T(8,128)S(1)}, f32[4096,128]{1,0:T(8,128)}, f32[4096,128]{1,0:T(8,128)}, s32[]{:T(128)}, /*index=5*/s32[512]{0:T(...) while((s32[]{:T(128)}, f32[512,128]{1,0:T(8,128)S(1)}, ...), condition=%wide.region_9.9_spmd, body=%wide.region_8.8_spmd.sunk | while | flops 338625024 | bytes 7225595 | solution.py:113
  306.7 4.6 all-to-all-start.5
  312.7 15.6 %all-to-all-done.5 = bf16[32,128,128]{2,1,0:T(8,128)(2,1)} async-done(((bf16[32,128,128]{2,1,0:T(8,128)(2,1)}), bf16[32,128,128]{2,1,0:T(8,128)(2,1)}, u32[]{:S(2)}, u32[]{:S(2)}) %all-to-all-start.5) | async-done | bytes 1048608 | tf_op jit(solution)/shard_map/all_to_all | solution.py:164
  328.3 4.5 all-to-all-start.7
  336.7 2.0 fusion.24
  338.7 11.0 %all-to-all-done.7 = bf16[32,128,128]{2,1,0:T(8,128)(2,1)} async-done(((bf16[32,128,128]{2,1,0:T(8,128)(2,1)}), bf16[32,128,128]{2,1,0:T(8,128)(2,1)}, u32[]{:S(2)}, u32[]{:S(2)}) %all-to-all-start.7) | async-done | bytes 1048608 | tf_op jit(solution)/shard_map/all_to_all | solution.py:166
  349.7 4.6 all-to-all-start.6
  356.0 2.0 fusion.25
  358.1 2.4 fusion.26
  361.8 30.4 %reduce-scatter.7.cloned.1.call-done = f32[8,512]{1,0:T(8,128)} async-done(((f32[8,4096]{1,0:T(8,128)}), f32[8,512]{1,0:T(8,128)}) %reduce-scatter.7.cloned.1.call-update) | async-done | bytes 16400 | tf_op jit(solution)/shard_map/reduce_scatter | solution.py:193
  392.2 37.8 %reduce-scatter.11.cloned.1.call-done = f32[8,512]{1,0:T(8,128)} async-done(((f32[8,4096]{1,0:T(8,128)}), f32[8,512]{1,0:T(8,128)}) %reduce-scatter.11.cloned.1.call-update) | async-done | bytes 16400 | tf_op jit(solution)/shard_map/reduce_scatter | solution.py:195
  430.0 38.3 %reduce-scatter.5.cloned.1.call-done = f32[8,640]{1,0:T(8,128)} async-done(((f32[8,5120]{1,0:T(8,128)}), f32[8,640]{1,0:T(8,128)}) %reduce-scatter.5.cloned.1.call-update) | async-done | bytes 20496 | tf_op jit(solution)/shard_map/reduce_scatter | solution.py:192
  468.4 38.5 %reduce-scatter.9.cloned.1.call-done = f32[8,640]{1,0:T(8,128)} async-done(((f32[8,5120]{1,0:T(8,128)}), f32[8,640]{1,0:T(8,128)}) %reduce-scatter.9.cloned.1.call-update) | async-done | bytes 20496 | tf_op jit(solution)/shard_map/reduce_scatter | solution.py:194
  512.4 109.9 %all-reduce.3.cloned.1.call-done = (f32[8,640]{1,0:T(8,128)}, f32[8,512]{1,0:T(8,128)}, f32[8,640]{1,0:T(8,128)}, f32[8,512]{1,0:T(8,128)}) async-done(((f32[8,640]{1,0:T(8,128)}, f32[8,512]{1,0:T(8,128)}, f32[8,640]{1,0:T(8,128)}, f32[8,512]{1,0:T(8,128)}), (f32[8,640]{1,0:T(8,128)}, f32[8,512]{1,0:T(8,128)}, f32[8,640]{1,0:T(8,128)}, f32[8,512]{1,0:T(8,128)})) %all-reduce.3.cloned.1.call-update) | async-done | bytes 73744 | tf_op jit(solution)/shard_map/psum | solution.py:190
  (386 shorter events, 173.6 us)
Async XLA Ops:
  7.2 329.0 %copy-start = (bf16[128,5120]{1,0:T(8,128)(2,1)S(1)}, bf16[128,5120]{1,0:T(8,128)(2,1)}, u32[]{:S(2)}) copy-start(bf16[128,5120]{1,0:T(8,128)(2,1)} %param.17) | copy-start | bytes 3932164
  7.2 11.2 %copy-start.5 = (bf16[128,4096]{1,0:T(8,128)(2,1)S(1)}, bf16[128,4096]{1,0:T(8,128)(2,1)}, u32[]{:S(2)}) copy-start(bf16[128,4096]{1,0:T(8,128)(2,1)} %param.19) | copy-start | bytes 3145732
  9.8 25.5 %all-to-all-start = ((bf16[128,32,128]{2,0,1:T(8,128)(2,1)}), bf16[128,32,128]{2,0,1:T(8,128)(2,1)S(1)}, u32[]{:S(2)}, u32[]{:S(2)}) async-start(bf16[128,32,128]{2,0,1:T(8,128)(2,1)} %copy_bitcast_fusion.4), calls=%async_computation | async-start | bytes 2097152 | tf_op jit(solution)/shard_map/all_to_all | solution.py:152
  35.3 1.0 copy-start.4
  36.3 20.9 %all-to-all-start.1 = ((bf16[128,32,128]{2,0,1:T(8,128)(2,1)}), bf16[128,32,128]{2,0,1:T(8,128)(2,1)S(1)}, u32[]{:S(2)}, u32[]{:S(2)}) async-start(bf16[128,32,128]{2,0,1:T(8,128)(2,1)} %copy_bitcast_fusion.3), calls=%async_computation.1 | async-start | bytes 2097152 | tf_op jit(solution)/shard_map/all_to_all | solution.py:153
  57.2 21.4 %all-to-all-start.2 = ((bf16[128,32,128]{2,0,1:T(8,128)(2,1)}), bf16[128,32,128]{2,0,1:T(8,128)(2,1)}, u32[]{:S(2)}, u32[]{:S(2)}) async-start(bf16[128,32,128]{2,0,1:T(8,128)(2,1)} %copy_bitcast_fusion.2), calls=%async_computation.2 | async-start | bytes 2097152 | tf_op jit(solution)/shard_map/all_to_all | solution.py:156
  61.6 21.4 %copy-start.10 = (s32[1,4]{1,0:T(1,128)S(1)}, s32[1,4]{1,0:T(1,128)}, u32[]{:S(2)}) copy-start(s32[1,4]{1,0:T(1,128)} %param.23) | copy-start | bytes 52
  78.6 21.4 %all-to-all-start.3 = ((bf16[128,32,128]{2,0,1:T(8,128)(2,1)}), bf16[128,32,128]{2,0,1:T(8,128)(2,1)}, u32[]{:S(2)}, u32[]{:S(2)}) async-start(bf16[128,32,128]{2,0,1:T(8,128)(2,1)} %copy_bitcast_fusion.1), calls=%async_computation.3 | async-start | bytes 2097152 | tf_op jit(solution)/shard_map/all_to_all | solution.py:155
  100.1 21.4 %all-to-all-start.4 = ((bf16[128,32,128]{2,0,1:T(8,128)(2,1)}), bf16[128,32,128]{2,0,1:T(8,128)(2,1)}, u32[]{:S(2)}, u32[]{:S(2)}) async-start(bf16[128,32,128]{2,0,1:T(8,128)(2,1)} %copy_bitcast_fusion), calls=%async_computation.4 | async-start | bytes 2097152 | tf_op jit(solution)/shard_map/all_to_all | solution.py:154
  306.7 4.9 copy-start.1
  306.7 21.6 %all-to-all-start.5 = ((bf16[32,128,128]{2,1,0:T(8,128)(2,1)}), bf16[32,128,128]{2,1,0:T(8,128)(2,1)}, u32[]{:S(2)}, u32[]{:S(2)}) async-start(bf16[32,128,128]{2,1,0:T(8,128)(2,1)} %bitcast.152), calls=%async_computation.5 | async-start | bytes 2097152 | tf_op jit(solution)/shard_map/all_to_all | solution.py:164
  312.7 20.1 %copy-start.2 = (f32[4096,128]{1,0:T(8,128)S(1)}, f32[4096,128]{1,0:T(8,128)}, u32[]{:S(2)}) copy-start(f32[4096,128]{1,0:T(8,128)} %get-tuple-element.420) | copy-start | bytes 6291460
  328.3 21.4 %all-to-all-start.7 = ((bf16[32,128,128]{2,1,0:T(8,128)(2,1)}), bf16[32,128,128]{2,1,0:T(8,128)(2,1)}, u32[]{:S(2)}, u32[]{:S(2)}) async-start(bf16[32,128,128]{2,1,0:T(8,128)(2,1)} %bitcast.151), calls=%async_computation.7 | async-start | bytes 2097152 | tf_op jit(solution)/shard_map/all_to_all | solution.py:166
  332.7 59.5 %reduce-scatter.7.cloned.1.call-start = ((), (), s32[]{:S(2)}) async-start(), calls=%async_computation.13 | async-start | bytes 147456 | tf_op jit(solution)/shard_map/reduce_scatter | solution.py:193
  335.8 0.9 copy-start.6
  336.2 18.1 %copy-start.3 = (bf16[128,32,128]{0,2,1:T(8,128)(2,1)}, bf16[128,32,128]{0,2,1:T(8,128)(2,1)S(1)}, u32[]{:S(2)}) copy-start(bf16[128,32,128]{0,2,1:T(8,128)(2,1)S(1)} %pad_maximum_fusion) | copy-start | bytes 3145732
  349.7 6.3 copy-start.7
  349.7 159.8 %all-to-all-start.6 = ((bf16[32,128,128]{2,1,0:T(8,128)(2,1)}), bf16[32,128,128]{2,1,0:T(8,128)(2,1)}, u32[]{:S(2)}, u32[]{:S(2)}) async-start(bf16[32,128,128]{2,1,0:T(8,128)(2,1)} %bitcast.150), calls=%async_computation.6 | async-start | bytes 2097152 | tf_op jit(solution)/shard_map/all_to_all | solution.py:165
  354.3 3.8 copy-start.8
  354.3 75.7 %reduce-scatter.11.cloned.1.call-start = ((), (), s32[]{:S(2)}) async-start(), calls=%async_computation.15 | async-start | bytes 147456 | tf_op jit(solution)/shard_map/reduce_scatter | solution.py:195
  358.0 2.6 copy-start.9
  358.0 110.4 %reduce-scatter.5.cloned.1.call-start = ((), (), s32[]{:S(2)}) async-start(), calls=%async_computation.12 | async-start | bytes 184320 | tf_op jit(solution)/shard_map/reduce_scatter | solution.py:192
  360.5 146.3 %reduce-scatter.9.cloned.1.call-start = ((), (), s32[]{:S(2)}) async-start(), calls=%async_computation.14 | async-start | bytes 184320 | tf_op jit(solution)/shard_map/reduce_scatter | solution.py:194
  361.8 260.5 %all-reduce.3.cloned.1.call-start = ((), (), s32[]{:S(2)}) async-start(), calls=%async_computation.16 | async-start | bytes 147456 | tf_op jit(solution)/shard_map/psum | solution.py:190
Sparse Core Ops, SparseCore 0:
  338.8 53.3 reduce-scatter.6
  394.8 35.1 reduce-scatter.10
  433.1 35.2 reduce-scatter.4
  471.4 35.3 reduce-scatter.8
  510.4 111.8 all-reduce.2
where the time goes:
time: 628 us; the launch traced here: 631 us
  waiting for transfers between devices  354 us (56%)
  matrix products  140 us (22%)
  starting transfers between devices  39.7 us (6%)
  local copies, waits for them, and re-layouts  38.1 us (6%)
  loops' own time  23.1 us (4%)
  other arithmetic  22.1 us (4%)
  between operations  14.1 us (2%)
    psum x1, waiting for transfers between devices, shards(): summed = lax.psum((terms[0], terms[1], terms[2], terms[3]), 'seq')  110 us
    dot_general x21, matrix products, gradients(): jnp.dot(grad_score.T, query_rows, preferred_element_type=jnp.float32)  41 us
    dot_general x21, matrix products, gradients(): jnp.dot(prob_low.T, grad_rows, preferred_element_type=jnp.float32)  41 us
    reduce_scatter x1, waiting for transfers between devices, shards(): lax.psum_scatter(summed[2], 'dp', scatter_dimension=1, tiled=True)  38.5 us
    reduce_scatter x1, waiting for transfers between devices, shards(): lax.psum_scatter(summed[0], 'dp', scatter_dimension=1, tiled=True)  38.3 us
    reduce_scatter x1, waiting for transfers between devices, shards(): lax.psum_scatter(summed[3], 'dp', scatter_dimension=1, tiled=True)  37.8 us
    reduce_scatter x1, waiting for transfers between devices, shards(): lax.psum_scatter(summed[1], 'dp', scatter_dimension=1, tiled=True)  30.4 us
    dot_general x21, matrix products, gradients(): jnp.dot(grad_rows, value_rows.T, preferred_element_type=jnp.float32)  25.3 us
  transfers between devices with their start and end apart: 13, of which 12 were waited for; matrix products, arithmetic and copies ran while one was open for 5% of the time, Pallas kernels for 0%

commit v1 on v0

v1 whole, which is shorter than its diff:
```python
import math

import jax
import jax.numpy as jnp
from jax import lax
from jax.experimental import pallas as pl
from jax.experimental.pallas import tpu as pltpu
from jax.sharding import PartitionSpec as P

H = 32
HD = 128
RANK = 8
ADAPTER_SCALE = 2.0
BQ = 256
BK = 256
MESH = pl.DeviceIdType.MESH
NT = (((1,), (1,)), ((), ()))
F32 = jnp.float32
BF16 = jnp.bfloat16


def nt_dot(a, b):
    return lax.dot_general(a, b, NT, preferred_element_type=F32)


def starts_of(len_ref):
    first = len_ref[0, 0]
    second = first + len_ref[0, 1]
    third = second + len_ref[0, 2]
    return first, second, third


def begin_of(positions, starts):
    found = jnp.zeros_like(positions)
    for start in starts:
        found = jnp.where(positions >= start, start, found)
    return found


def partner(me, step):
    return lax.rem(me + step, 32)


def gather_kernel(q_ref, k_ref, v_ref, g_ref, o_ref, hq, hk, hv, hg, hd, g_buf, o_buf, d_buf, send, recv, local, load):
    members = 32
    me = lax.axis_index("seq")
    rows = q_ref.shape[0]
    barrier = pltpu.get_barrier_semaphore()

    def greet(step, _):
        pl.semaphore_signal(barrier, inc=1, device_id={"seq": partner(me, step)}, device_id_type=MESH)
        return 0

    lax.fori_loop(1, members, greet, 0)
    load_g = pltpu.make_async_copy(g_ref, g_buf, load.at[0])
    load_o = pltpu.make_async_copy(o_ref, o_buf, load.at[1])
    load_g.start()
    load_o.start()
    pairs = ((q_ref, hq), (k_ref, hk), (v_ref, hv), (g_ref, hg))
    my_rows = pl.ds(pl.multiple_of(me * rows, rows), rows)

    def columns(member):
        return pl.ds(pl.multiple_of(member * HD, HD), HD)

    own = [
        pltpu.make_async_copy(src.at[:, columns(me)], dst.at[my_rows, :], local.at[index])
        for index, (src, dst) in enumerate(pairs)
    ]
    for copy in own:
        copy.start()
    pl.semaphore_wait(barrier, members - 1)

    def remote(index, step):
        src, dst = pairs[index]
        other = partner(me, step)
        return pltpu.make_async_remote_copy(
            src_ref=src.at[:, columns(other)],
            dst_ref=dst.at[my_rows, :],
            send_sem=send.at[index, step],
            recv_sem=recv.at[index, step],
            device_id={"seq": other},
            device_id_type=MESH,
        )

    def remote_delta(step):
        other = partner(me, step)
        return pltpu.make_async_remote_copy(
            src_ref=d_buf.at[other],
            dst_ref=hd.at[me],
            send_sem=send.at[4, step],
            recv_sem=recv.at[4, step],
            device_id={"seq": other},
            device_id_type=MESH,
        )

    def start_all(step, _):
        for index in range(4):
            remote(index, step).start()
        return 0

    lax.fori_loop(1, members, start_all, 0)
    load_g.wait()
    load_o.wait()

    def delta_of(head, _):
        cols = columns(head)
        product = g_buf[:, cols].astype(F32) * o_buf[:, cols].astype(F32)
        d_buf[head] = jnp.sum(product.T, axis=0, keepdims=True)
        return 0

    lax.fori_loop(0, H, delta_of, 0)
    own_delta = pltpu.make_async_copy(d_buf.at[me], hd.at[me], local.at[4])
    own_delta.start()

    def start_delta(step, _):
        remote_delta(step).start()
        return 0

    lax.fori_loop(1, members, start_delta, 0)
    for copy in own:
        copy.wait()
    own_delta.wait()

    def finish(step, _):
        for index in range(4):
            remote(index, step).wait()
        remote_delta(step).wait()
        return 0

    lax.fori_loop(1, members, finish, 0)


def gather_heads(queries, key_states, value_states, grad_out, attention_out):
    rows, width = queries.shape
    anywhere = pl.BlockSpec(memory_space=pl.ANY)
    total = rows * 32
    head = jax.ShapeDtypeStruct((total, HD), BF16)
    return pl.pallas_call(
        gather_kernel,
        name="gather_heads",
        out_shape=(head, head, head, head, jax.ShapeDtypeStruct((32, 1, rows), F32)),
        in_specs=[anywhere] * 5,
        out_specs=[anywhere] * 5,
        scratch_shapes=[
            pltpu.VMEM((rows, width), BF16),
            pltpu.VMEM((rows, width), BF16),
            pltpu.VMEM((H, 1, rows), F32),
            pltpu.SemaphoreType.DMA((5, 32)),
            pltpu.SemaphoreType.DMA((5, 32)),
            pltpu.SemaphoreType.DMA((5,)),
            pltpu.SemaphoreType.DMA((2,)),
        ],
        compiler_params=pltpu.CompilerParams(
            collective_id=0, has_side_effects=True, vmem_limit_bytes=16 << 20
        ),
    )(queries, key_states, value_states, grad_out, attention_out)


def attention_kernel(len_ref, q_ref, k_ref, v_ref, g_ref, d_ref, dq_ref, dk_ref, dv_ref, kt, w_buf, t_buf, dk_acc, dv_acc, stat):
    total = q_ref.shape[0]
    starts = starts_of(len_ref)
    scaling = 1.0 / math.sqrt(HD)
    to_log2 = scaling * math.log2(math.e)
    dk_acc[...] = jnp.zeros_like(dk_acc)
    dv_acc[...] = jnp.zeros_like(dv_acc)

    def turn(block, _):
        at = pl.multiple_of(block * 256, 256)
        kt[:, pl.ds(at, 256)] = k_ref[pl.ds(at, 256), :].T
        return 0

    lax.fori_loop(0, total // 256, turn, 0)

    def fold(x, op):
        return op(x.reshape(x.shape[0] // 8, 8, x.shape[1]), axis=0)

    def outer(query_block, _):
        q0 = pl.multiple_of(query_block * BQ, BQ)
        q_rows = q_ref[pl.ds(q0, BQ), :]
        g_rows = g_ref[pl.ds(q0, BQ), :]
        delta = jnp.concatenate([d_ref[query_block * (BQ // 128) + i] for i in range(BQ // 128)], axis=1)
        query_at = q0 + lax.broadcasted_iota(jnp.int32, (1, BQ), 1)
        query_begin = begin_of(query_at, starts)
        low = begin_of(q0, starts)
        high = begin_of(q0 + (BQ - 1), starts)
        first = lax.div(low, BK)
        last = lax.div(q0 + (BQ - 1), BK) + 1
        stat[0] = jnp.full((8, BQ), -1e30, F32)

        def score(key_block, _):
            k0 = pl.multiple_of(key_block * BK, BK)
            rows = pl.ds(k0, BK)
            inside = jnp.logical_and(high <= k0, k0 + (BK - 1) <= q0)

            @pl.when(inside)
            def _():
                s = nt_dot(k_ref[rows, :], q_rows)
                w_buf[rows, :] = s
                stat[0] = jnp.maximum(stat[0], fold(s, jnp.max))

            @pl.when(jnp.logical_not(inside))
            def _():
                key_at = k0 + lax.broadcasted_iota(jnp.int32, (BK, BQ), 0)
                allowed = jnp.logical_and(key_at >= query_begin, key_at <= query_at)
                s = jnp.where(allowed, nt_dot(k_ref[rows, :], q_rows), -1e30)
                w_buf[rows, :] = s
                stat[0] = jnp.maximum(stat[0], fold(s, jnp.max))

            return 0

        lax.fori_loop(first, last, score, 0)
        top = jnp.max(stat[0], axis=0, keepdims=True)
        stat[1] = jnp.zeros((8, BQ), F32)

        def weigh(key_block, _):
            rows = pl.ds(pl.multiple_of(key_block * BK, BK), BK)
            w = jnp.exp2((w_buf[rows, :] - top) * to_log2)
            stat[1] = stat[1] + fold(w, jnp.sum)
            w_buf[rows, :] = w
            t_buf[rows, :] = w * (nt_dot(v_ref[rows, :], g_rows) - delta)
            return 0

        lax.fori_loop(first, last, weigh, 0)
        inverse = 1.0 / jnp.sum(stat[1], axis=0, keepdims=True)

        def spread(key_block, dq):
            k0 = pl.multiple_of(key_block * BK, BK)
            rows = pl.ds(k0, BK)
            p = (w_buf[rows, :] * inverse).astype(BF16)
            ds = (t_buf[rows, :] * inverse).astype(BF16)
            dv_acc[rows, :] += jnp.dot(p, g_rows, preferred_element_type=F32)
            dk_acc[rows, :] += jnp.dot(ds, q_rows, preferred_element_type=F32)
            return dq + jnp.dot(kt[:, rows], ds, preferred_element_type=F32)

        dq = lax.fori_loop(first, last, spread, jnp.zeros((HD, BQ), F32))
        dq_ref[pl.ds(q0, BQ), :] = (dq * scaling).T.astype(BF16)
        return 0

    lax.fori_loop(0, total // BQ, outer, 0)
    dk_ref[...] = (dk_acc[...] * scaling).astype(BF16)
    dv_ref[...] = dv_acc[...].astype(BF16)


def attention_backward(lengths, q, k, v, g, delta):
    total = q.shape[0]
    vmem = pl.BlockSpec(memory_space=pltpu.VMEM)
    head = jax.ShapeDtypeStruct((total, HD), BF16)
    return pl.pallas_call(
        attention_kernel,
        name="attention_backward",
        out_shape=(head, head, head),
        in_specs=[pl.BlockSpec(memory_space=pltpu.SMEM)] + [vmem] * 5,
        out_specs=[vmem] * 3,
        scratch_shapes=[
            pltpu.VMEM((HD, total), BF16),
            pltpu.VMEM((total, BQ), F32),
            pltpu.VMEM((total, BQ), F32),
            pltpu.VMEM((total, HD), F32),
            pltpu.VMEM((total, HD), F32),
            pltpu.VMEM((2, 8, BQ), F32),
        ],
        compiler_params=pltpu.CompilerParams(vmem_limit_bytes=48 << 20),
    )(lengths, q, k, v, g, delta)


def adapter_kernel(
    len_ref, dq_ref, dk_ref, dv_ref, hid_ref, downq, upq, downv, upv,
    gq_ref, gk_ref, gv_ref, qd_ref, qu_ref, vd_ref, vu_ref,
    q_in, v_in, turned, hid, part, z_in, tiles, r_in, done,
    send, recv, local, load, z_send, z_recv, r_send, r_recv, a_send, a_recv,
):
    members, groups = 32, 8
    me = lax.axis_index("seq")
    dp = lax.axis_index("dp")
    rows, width = q_in.shape
    model = hid.shape[1]
    d_cols = model // groups
    u_cols = width // groups
    d_tiles = d_cols // 128
    u_tiles = u_cols // 128
    n_tiles = 2 * (d_tiles + u_tiles)
    barrier = pltpu.get_barrier_semaphore()

    def across(step):
        return lax.rem(dp + step, groups)

    def greet(step, _):
        pl.semaphore_signal(barrier, inc=1, device_id={"seq": partner(me, step)}, device_id_type=MESH)
        return 0

    def greet_group(step, _):
        pl.semaphore_signal(barrier, inc=1, device_id={"dp": across(step)}, device_id_type=MESH)
        return 0

    lax.fori_loop(1, members, greet, 0)
    lax.fori_loop(1, groups, greet_group, 0)
    load_hid = pltpu.make_async_copy(hid_ref, hid, load.at[0])
    load_hid.start()
    pairs = ((dq_ref, q_in), (dv_ref, v_in), (dk_ref, gk_ref))
    my_cols = pl.ds(pl.multiple_of(me * HD, HD), HD)

    def rows_of(member):
        return pl.ds(pl.multiple_of(member * rows, rows), rows)

    own = [
        pltpu.make_async_copy(src.at[rows_of(me), :], dst.at[:, my_cols], local.at[index])
        for index, (src, dst) in enumerate(pairs)
    ]
    for copy in own:
        copy.start()
    pl.semaphore_wait(barrier, members - 1 + groups - 1)

    def remote(index, step):
        src, dst = pairs[index]
        other = partner(me, step)
        return pltpu.make_async_remote_copy(
            src_ref=src.at[rows_of(other), :],
            dst_ref=dst.at[:, my_cols],
            send_sem=send.at[index, step],
            recv_sem=recv.at[index, step],
            device_id={"seq": other},
            device_id_type=MESH,
        )

    for index in range(3):
        def start_one(step, _, index=index):
            remote(index, step).start()
            return 0

        lax.fori_loop(1, members, start_one, 0)

    load_hid.wait()
    low_q = nt_dot(downq[...], hid[...]).astype(BF16)
    low_v = nt_dot(downv[...], hid[...]).astype(BF16)
    token = me * rows + lax.broadcasted_iota(jnp.int32, (rows, HD), 0)
    place = (token - begin_of(token, starts_of(len_ref))).astype(F32)
    lane = lax.broadcasted_iota(jnp.int32, (rows, HD), 1)
    pair = jnp.where(lane >= HD // 2, lane - HD // 2, lane).astype(F32)
    angle = place * jnp.exp(-(pair * (2.0 / HD)) * math.log(10000.0))
    cosine = jnp.cos(angle)
    sine = jnp.sin(angle)
    sine = jnp.where(lane >= HD // 2, -sine, sine)
    for copy in own:
        copy.wait()

    def finish_q(step, _):
        remote(0, step).wait_recv()
        return 0

    def finish_v(step, _):
        remote(1, step).wait_recv()
        return 0

    lax.fori_loop(1, members, finish_q, 0)
    save_q = pltpu.make_async_copy(q_in, gq_ref, load.at[1])
    save_q.start()
    for head in range(H):
        cols = slice(head * HD, (head + 1) * HD)
        x = q_in[:, cols].astype(F32)
        turned[:, cols] = (x * cosine + pltpu.roll(x, HD // 2, 1) * sine).astype(BF16)
    back_q = nt_dot(upq[...], turned[...]).astype(BF16)
    lax.fori_loop(1, members, finish_v, 0)
    save_v = pltpu.make_async_copy(v_in, gv_ref, load.at[2])
    save_v.start()
    back_v = nt_dot(upv[...], v_in[...]).astype(BF16)
    for group in range(groups):
        cols = slice(group * d_cols, (group + 1) * d_cols)
        part[group, 0:8, 0:d_cols] = jnp.dot(back_q, hid[:, cols], preferred_element_type=F32)
        part[group, 8:16, 0:d_cols] = jnp.dot(back_v, hid[:, cols], preferred_element_type=F32)
        cols = slice(group * u_cols, (group + 1) * u_cols)
        part[group, 0:8, d_cols:] = jnp.dot(low_q, turned[:, cols], preferred_element_type=F32)
        part[group, 8:16, d_cols:] = jnp.dot(low_v, v_in[:, cols], preferred_element_type=F32)

    def exchange(step):
        other = across(step)
        return pltpu.make_async_remote_copy(
            src_ref=part.at[other],
            dst_ref=z_in.at[step],
            send_sem=z_send.at[step],
            recv_sem=z_recv.at[step],
            device_id={"dp": other},
            device_id_type=MESH,
        )

    for step in range(1, groups):
        exchange(step).start()
    total = part[dp]
    for step in range(1, groups):
        exchange(step).wait()
        total = total + z_in[step]
    for tile in range(n_tiles):
        column, half = tile // 2, tile % 2
        tiles[tile] = total[half * 8:half * 8 + 8, column * 128:(column + 1) * 128]

    def scatter(step):
        other = partner(me, step)
        return other, pltpu.make_async_remote_copy(
            src_ref=tiles.at[lax.rem(other, n_tiles)],
            dst_ref=r_in.at[step],
            send_sem=r_send.at[step],
            recv_sem=r_recv.at[step],
            device_id={"seq": other},
            device_id_type=MESH,
        )

    def spread(step):
        return pltpu.make_async_remote_copy(
            src_ref=done.at[lax.rem(me, n_tiles)],
            dst_ref=done.at[lax.rem(me, n_tiles)],
            send_sem=a_send.at[step],
            recv_sem=a_recv.at[step],
            device_id={"seq": partner(me, step)},
            device_id_type=MESH,
        )

    def collect(step):
        sender = lax.rem(me + members - step, members)
        return sender, pltpu.make_async_remote_copy(
            src_ref=done.at[lax.rem(sender, n_tiles)],
            dst_ref=done.at[lax.rem(sender, n_tiles)],
            send_sem=a_send.at[step],
            recv_sem=a_recv.at[step],
            device_id={"seq": partner(me, step)},
            device_id_type=MESH,
        )

    def start_scatter(step, _):
        other, copy = scatter(step)

        @pl.when(other < n_tiles)
        def _():
            copy.start()

        return 0

    lax.fori_loop(1, members, start_scatter, 0)

    @pl.when(me < n_tiles)
    def _():
        def wait_scatter(step, _):
            scatter(step)[1].wait_recv()
            return 0

        lax.fori_loop(1, members, wait_scatter, 0)
        summed = tiles[me]
        for step in range(1, members):
            summed = summed + r_in[step]
        done[me] = summed * ADAPTER_SCALE

        def start_spread(step, _):
            spread(step).start()
            return 0

        lax.fori_loop(1, members, start_spread, 0)

    def wait_spread(step, _):
        sender, copy = collect(step)

        @pl.when(sender < n_tiles)
        def _():
            copy.wait_recv()

        return 0

    lax.fori_loop(1, members, wait_spread, 0)
    for column in range(d_tiles):
        cols = slice(column * 128, (column + 1) * 128)
        qd_ref[:, cols] = done[2 * column]
        vd_ref[:, cols] = done[2 * column + 1]
    for column in range(u_tiles):
        cols = slice(column * 128, (column + 1) * 128)
        qu_ref[:, cols] = done[2 * (d_tiles + column)]
        vu_ref[:, cols] = done[2 * (d_tiles + column) + 1]

    def finish(step, _):
        remote(0, step).wait_send()
        remote(1, step).wait_send()
        remote(2, step).wait()
        other, copy = scatter(step)

        @pl.when(other < n_tiles)
        def _():
            copy.wait_send()

        @pl.when(me < n_tiles)
        def _():
            spread(step).wait_send()

        return 0

    lax.fori_loop(1, members, finish, 0)
    save_q.wait()
    save_v.wait()


def adapters(lengths, dq, dk, dv, hidden, down_query, up_query, down_value, up_value):
    rows, model = hidden.shape
    width = up_query.shape[1]
    anywhere = pl.BlockSpec(memory_space=pl.ANY)
    vmem = pl.BlockSpec(memory_space=pltpu.VMEM)
    grad = jax.ShapeDtypeStruct((rows, width), BF16)
    down = jax.ShapeDtypeStruct((RANK, model // 8), F32)
    up = jax.ShapeDtypeStruct((RANK, width // 8), F32)
    each = (model + width) // 8
    n_tiles = 2 * each // 128
    dma = pltpu.SemaphoreType.DMA
    return pl.pallas_call(
        adapter_kernel,
        name="return_and_adapters",
        out_shape=(grad, grad, grad, down, up, down, up),
        in_specs=[pl.BlockSpec(memory_space=pltpu.SMEM)] + [anywhere] * 4 + [vmem] * 4,
        out_specs=[anywhere] * 3 + [vmem] * 4,
        scratch_shapes=[
            pltpu.VMEM((rows, width), BF16),
            pltpu.VMEM((rows, width), BF16),
            pltpu.VMEM((rows, width), BF16),
            pltpu.VMEM((rows, model), BF16),
            pltpu.VMEM((8, 2 * RANK, each), F32),
            pltpu.VMEM((8, 2 * RANK, each), F32),
            pltpu.VMEM((n_tiles, 8, 128), F32),
            pltpu.VMEM((32, 8, 128), F32),
            pltpu.VMEM((n_tiles, 8, 128), F32),
            dma((3, 32)),
            dma((3, 32)),
            dma((3,)),
            dma((3,)),
            dma((8,)),
            dma((8,)),
            dma((32,)),
            dma((32,)),
            dma((32,)),
            dma((32,)),
        ],
        compiler_params=pltpu.CompilerParams(
            collective_id=1, has_side_effects=True, vmem_limit_bytes=32 << 20
        ),
    )(lengths, dq, dk, dv, hidden, down_query, up_query, down_value, up_value)


def shards(
    hidden,
    queries,
    key_states,
    value_states,
    attention_out,
    grad_out,
    lengths,
    down_query,
    up_query,
    down_value,
    up_value,
):
    q, k, v, g, delta = gather_heads(queries, key_states, value_states, grad_out, attention_out)
    dq, dk, dv = attention_backward(lengths, q, k, v, g, delta)
    return adapters(lengths, dq, dk, dv, hidden, down_query, up_query, down_value, up_value)


def solution(mesh):
    tokens = P(("dp", "seq"), None)
    return jax.shard_map(
        shards,
        mesh=mesh,
        in_specs=(tokens,) * 6 + (P("dp", None), P(), P(), P(), P()),
        out_specs=(tokens,) * 3 + (P(None, "dp"),) * 4,
        check_vma=False,
    )
```

time: 628 us -> 235 us (0.37)
  waiting for transfers between devices: 354 us -> 0 us
  Pallas kernels: 0 us -> 219 us
  matrix products: 140 us -> 0 us
  starting transfers between devices: 39.7 us -> 0 us
  local copies, waits for them, and re-layouts: 38.1 us -> 13.4 us
  loops' own time: 23.1 us -> 0 us
  other arithmetic: 22.1 us -> 0 us
  between operations: 14.1 us -> 0.74 us
    pallas_call x0 -> x3, Pallas kernels: none -> 219 us  [the longest x1 89.4 us: adapters(): pl.pallas_call(adapter_kernel, name='return_and_adapters', out_shape=(gra...]
    reduce_scatter x4 -> x0, waiting for transfers between devices: 145 us -> none  [the longest x1 38.5 us: shards(): lax.psum_scatter(summed[2], 'dp', scatter_dimension=1, tiled=True)]
    dot_general x130 -> x0, matrix products: 140 us -> none  [the longest x21 41 us: gradients(): jnp.dot(grad_score.T, query_rows, preferred_element_type=jnp.float32)]
    psum x1 -> x0, waiting for transfers between devices: 110 us -> none  [shards(): summed = lax.psum((terms[0], terms[1], terms[2], terms[3]), 'seq')]
    all_to_all x8 -> x0, waiting for transfers between devices: 99.1 us -> none  [the longest x1 15.6 us: shards(): lax.all_to_all(queries, 'seq', split_axis=1, concat_axis=0, tiled=True)]
    all_to_all x8 -> x0, starting transfers between devices: 39.5 us -> none  [the longest x1 8.59 us: shards(): lax.all_to_all(queries, 'seq', split_axis=1, concat_axis=0, tiled=True)]
    another operation x17 -> x0, loops' own time: 23.1 us -> none  [the longest x1 21.2 us: head_backward(): lax.fori_loop(0, block_count, outer, (empty_rows, empty_rows, empty_rows))]
    all_to_all x8 -> x0, local copies, waits for them, and re-layouts: 16.2 us -> none  [the longest x1 2.64 us: shards(): lax.all_to_all(queries, 'seq', split_axis=1, concat_axis=0, tiled=True)]
  transfers between devices with their start and end apart: 13 -> 0, of which waited for: 12 -> 0; matrix products, arithmetic and copies ran while one was open for 5% -> 0% of each run, Pallas kernels for 0% -> 0%
where the time goes in v1:
time: 235 us; the launch traced here: 234 us
  Pallas kernels  219 us (93%)
  local copies, waits for them, and re-layouts  13.4 us (6%)
    pallas_call x1, Pallas kernels, adapters(): pl.pallas_call(adapter_kernel, name='return_and_adapters', out_shape=(gra...  89.4 us
    pallas_call x1, Pallas kernels, gather_heads(): pl.pallas_call(gather_kernel, name='gather_heads', out_shape=(head, head,...  88.7 us
    pallas_call x1, Pallas kernels, attention_backward(): pl.pallas_call(attention_kernel, name='attention_backward', out_shape=(he...  41.4 us
    unnamed x33, local copies, waits for them, and re-layouts  13.4 us

profile of v1, /device:TPU:1, one launch (start us, length us, event | category | flops | bytes accessed | tf_op | source)
XLA Modules:
  0.0 233.6 jit_solution(12904867691066668539)
XLA Ops:
  0.6 0.0 copy-start.1
  0.6 1.2 copy-done.1
  1.9 0.0 copy-start.2
  1.9 1.2 copy-done.2
  3.1 0.0 copy-start.3
  3.1 1.2 copy-done.3
  4.3 0.0 copy-start.4
  4.3 1.2 copy-done.4
  5.5 0.0 copy-start.5
  5.5 1.2 copy-done.5
  6.8 0.0 copy-start.12
  6.8 88.7 %gather_heads.1 = (bf16[4096,128]{1,0:T(8,128)(2,1)S(1)}, bf16[4096,128]{1,0:T(8,128)(2,1)S(1)}, bf16[4096,128]{1,0:T(8,128)(2,1)S(1)}, bf16[4096,128]{1,0:T(8,128)(2,1)S(1)}, f32[32,1,128]{2,1,0:T(1,128)S(1)}) custom-call(bf16[128,4096]{1,0:T(8,128)(2,1)S(1)} %copy-done.1, bf16[128,4096]{1,0:T(8,128)(2,1)S(1)} %copy-done.2, ...), custom_call_target="tpu_custom_call" | custom-call | tf_op jit(solution)/shard_map/gather_heads/pallas_call | solution.py:138
  95.4 0.0 copy-start.6
  95.4 1.0 copy-done.6
  96.4 0.0 copy-start.7
  96.4 1.0 copy-done.7
  97.4 0.0 copy-done.12
  97.4 0.0 copy-start
  97.4 0.0 copy-start.8
  97.4 0.0 copy-start.9
  97.4 0.0 copy-start.10
  97.4 0.0 copy-start.11
  97.4 41.4 %attention_backward.1 = (bf16[4096,128]{1,0:T(8,128)(2,1)S(1)}, bf16[4096,128]{1,0:T(8,128)(2,1)S(1)}, bf16[4096,128]{1,0:T(8,128)(2,1)S(1)}) custom-call(s32[1,4]{1,0:T(1,128)S(1)} %copy-done.12, bf16[4096,128]{1,0:T(8,128)(2,1)S(1)} %get-tuple-element.15.q_ref, bf16[4096,128]{1,0:T(8,128)(2,1)S(1)} %get-tuple-element.16.k_ref, ...), custom_call_target="tpu_custom_call" | custom-call | tf_op jit(solution)/shard_map/attention_backward/pallas_call | solution.py:248
  138.8 0.0 copy-done
  138.8 0.0 copy-done.8
  138.8 0.0 copy-done.9
  138.9 0.0 copy-done.10
  138.9 0.0 copy-done.11
  138.9 89.4 %return_and_adapters.1 = (bf16[128,4096]{1,0:T(8,128)(2,1)S(1)}, bf16[128,4096]{1,0:T(8,128)(2,1)S(1)}, bf16[128,4096]{1,0:T(8,128)(2,1)S(1)}, f32[8,640]{1,0:T(...) custom-call(s32[1,4]{1,0:T(1,128)S(1)} %copy-done.12, ...), custom_call_target="tpu_custom_call" | custom-call | tf_op jit(solution)/shard_map/return_and_adapters/pallas_call | solution.py:507
  228.3 1.0 copy.25
  229.3 1.0 copy.26
  230.2 1.0 copy.27
  231.2 0.6 copy.28
  231.8 0.6 copy.29
  232.4 0.6 copy.30
  233.0 0.6 copy.31
Async XLA Ops:
  0.6 1.2 copy-start.1
  1.9 1.2 copy-start.2
  3.1 1.2 copy-start.3
  4.3 1.2 copy-start.4
  5.5 1.2 copy-start.5
  6.8 90.6 %copy-start.12 = (s32[1,4]{1,0:T(1,128)S(1)}, s32[1,4]{1,0:T(1,128)}, u32[]{:S(2)}) copy-start(s32[1,4]{1,0:T(1,128)} %len_ref.3) | copy-start | bytes 52
  95.4 1.0 copy-start.6
  96.4 1.0 copy-start.7
  97.4 41.5 %copy-start = (bf16[128,5120]{1,0:T(8,128)(2,1)S(1)}, bf16[128,5120]{1,0:T(8,128)(2,1)}, u32[]{:S(2)}) copy-start(bf16[128,5120]{1,0:T(8,128)(2,1)} %hid_ref.1) | copy-start | bytes 3932164
  97.4 41.5 %copy-start.8 = (bf16[8,5120]{1,0:T(8,128)(2,1)S(1)}, bf16[8,5120]{1,0:T(8,128)(2,1)}, u32[]{:S(2)}) copy-start(bf16[8,5120]{1,0:T(8,128)(2,1)} %downq.1) | copy-start | bytes 245764
  97.4 41.5 %copy-start.9 = (bf16[8,5120]{1,0:T(8,128)(2,1)S(1)}, bf16[8,5120]{1,0:T(8,128)(2,1)}, u32[]{:S(2)}) copy-start(bf16[8,5120]{1,0:T(8,128)(2,1)} %downv.1) | copy-start | bytes 245764
  97.4 41.5 %copy-start.10 = (bf16[8,4096]{1,0:T(8,128)(2,1)S(1)}, bf16[8,4096]{1,0:T(8,128)(2,1)}, u32[]{:S(2)}) copy-start(bf16[8,4096]{1,0:T(8,128)(2,1)} %upq.1) | copy-start | bytes 196612
  97.4 41.5 %copy-start.11 = (bf16[8,4096]{1,0:T(8,128)(2,1)S(1)}, bf16[8,4096]{1,0:T(8,128)(2,1)}, u32[]{:S(2)}) copy-start(bf16[8,4096]{1,0:T(8,128)(2,1)} %upv.1) | copy-start | bytes 196612

commit v2 on v1

--- a/solution.py
+++ b/solution.py
@@ -11,8 +11,8 @@
 HD = 128
 RANK = 8
 ADAPTER_SCALE = 2.0
-BQ = 256
-BK = 256
+BQ = 512
+BK = 512
 MESH = pl.DeviceIdType.MESH
 NT = (((1,), (1,)), ((), ()))
 F32 = jnp.float32
@@ -38,7 +38,17 @@
 
 
 def partner(me, step):
-    return lax.rem(me + step, 32)
+    chip = lax.rem(lax.rem(step, 16) * 7, 16)
+    x = lax.rem(lax.div(me, 8) + lax.div(chip, 4), 4)
+    y = lax.rem(lax.div(me, 2) + lax.rem(chip, 4), 4)
+    return x * 8 + y * 2 + lax.rem(me + lax.div(step, 16), 2)
+
+
+def sender_of(me, step):
+    chip = lax.rem(lax.rem(step, 16) * 7, 16)
+    x = lax.rem(lax.div(me, 8) + 4 - lax.div(chip, 4), 4)
+    y = lax.rem(lax.div(me, 2) + 4 - lax.rem(chip, 4), 4)
+    return x * 8 + y * 2 + lax.rem(me + lax.div(step, 16), 2)
 
 
 def gather_kernel(q_ref, k_ref, v_ref, g_ref, o_ref, hq, hk, hv, hg, hd, g_buf, o_buf, d_buf, send, recv, local, load):
@@ -132,15 +142,16 @@
 
 def gather_heads(queries, key_states, value_states, grad_out, attention_out):
     rows, width = queries.shape
-    anywhere = pl.BlockSpec(memory_space=pl.ANY)
+    hbm = pl.BlockSpec(memory_space=pltpu.HBM)
+    vmem = pl.BlockSpec(memory_space=pltpu.VMEM)
     total = rows * 32
     head = jax.ShapeDtypeStruct((total, HD), BF16)
     return pl.pallas_call(
         gather_kernel,
         name="gather_heads",
         out_shape=(head, head, head, head, jax.ShapeDtypeStruct((32, 1, rows), F32)),
-        in_specs=[anywhere] * 5,
-        out_specs=[anywhere] * 5,
+        in_specs=[hbm] * 5,
+        out_specs=[vmem] * 5,
         scratch_shapes=[
             pltpu.VMEM((rows, width), BF16),
             pltpu.VMEM((rows, width), BF16),
@@ -151,7 +162,7 @@
             pltpu.SemaphoreType.DMA((2,)),
         ],
         compiler_params=pltpu.CompilerParams(
-            collective_id=0, has_side_effects=True, vmem_limit_bytes=16 << 20
+            collective_id=0, has_side_effects=True, vmem_limit_bytes=49 << 20
         ),
     )(queries, key_states, value_states, grad_out, attention_out)
 
@@ -259,19 +270,20 @@
             pltpu.VMEM((total, HD), F32),
             pltpu.VMEM((2, 8, BQ), F32),
         ],
-        compiler_params=pltpu.CompilerParams(vmem_limit_bytes=48 << 20),
+        compiler_params=pltpu.CompilerParams(vmem_limit_bytes=28 << 20),
     )(lengths, q, k, v, g, delta)
 
 
 def adapter_kernel(
     len_ref, dq_ref, dk_ref, dv_ref, hid_ref, downq, upq, downv, upv,
     gq_ref, gk_ref, gv_ref, qd_ref, qu_ref, vd_ref, vu_ref,
-    q_in, v_in, turned, hid, part, z_in, tiles, r_in, done,
+    turned, hid, part, z_in, tiles, r_in, done,
     send, recv, local, load, z_send, z_recv, r_send, r_recv, a_send, a_recv,
 ):
     members, groups = 32, 8
     me = lax.axis_index("seq")
     dp = lax.axis_index("dp")
+    q_in, v_in = gq_ref, gv_ref
     rows, width = q_in.shape
     model = hid.shape[1]
     d_cols = model // groups
@@ -352,16 +364,12 @@
         return 0
 
     lax.fori_loop(1, members, finish_q, 0)
-    save_q = pltpu.make_async_copy(q_in, gq_ref, load.at[1])
-    save_q.start()
     for head in range(H):
         cols = slice(head * HD, (head + 1) * HD)
         x = q_in[:, cols].astype(F32)
         turned[:, cols] = (x * cosine + pltpu.roll(x, HD // 2, 1) * sine).astype(BF16)
     back_q = nt_dot(upq[...], turned[...]).astype(BF16)
     lax.fori_loop(1, members, finish_v, 0)
-    save_v = pltpu.make_async_copy(v_in, gv_ref, load.at[2])
-    save_v.start()
     back_v = nt_dot(upv[...], v_in[...]).astype(BF16)
     for group in range(groups):
         cols = slice(group * d_cols, (group + 1) * d_cols)
@@ -414,7 +422,7 @@
         )
 
     def collect(step):
-        sender = lax.rem(me + members - step, members)
+        sender = sender_of(me, step)
         return sender, pltpu.make_async_remote_copy(
             src_ref=done.at[lax.rem(sender, n_tiles)],
             dst_ref=done.at[lax.rem(sender, n_tiles)],
@@ -489,14 +497,12 @@
         return 0
 
     lax.fori_loop(1, members, finish, 0)
-    save_q.wait()
-    save_v.wait()
 
 
 def adapters(lengths, dq, dk, dv, hidden, down_query, up_query, down_value, up_value):
     rows, model = hidden.shape
     width = up_query.shape[1]
-    anywhere = pl.BlockSpec(memory_space=pl.ANY)
+    hbm = pl.BlockSpec(memory_space=pltpu.HBM)
     vmem = pl.BlockSpec(memory_space=pltpu.VMEM)
     grad = jax.ShapeDtypeStruct((rows, width), BF16)
     down = jax.ShapeDtypeStruct((RANK, model // 8), F32)
@@ -508,11 +514,9 @@
         adapter_kernel,
         name="return_and_adapters",
         out_shape=(grad, grad, grad, down, up, down, up),
-        in_specs=[pl.BlockSpec(memory_space=pltpu.SMEM)] + [anywhere] * 4 + [vmem] * 4,
-        out_specs=[anywhere] * 3 + [vmem] * 4,
+        in_specs=[pl.BlockSpec(memory_space=pltpu.SMEM)] + [vmem] * 3 + [hbm] + [vmem] * 4,
+        out_specs=[vmem] * 7,
         scratch_shapes=[
-            pltpu.VMEM((rows, width), BF16),
-            pltpu.VMEM((rows, width), BF16),
             pltpu.VMEM((rows, width), BF16),
             pltpu.VMEM((rows, model), BF16),
             pltpu.VMEM((8, 2 * RANK, each), F32),
@@ -523,7 +527,7 @@
             dma((3, 32)),
             dma((3, 32)),
             dma((3,)),
-            dma((3,)),
+            dma((1,)),
             dma((8,)),
             dma((8,)),
             dma((32,)),
@@ -532,7 +536,7 @@
             dma((32,)),
         ],
         compiler_params=pltpu.CompilerParams(
-            collective_id=1, has_side_effects=True, vmem_limit_bytes=32 << 20
+            collective_id=1, has_side_effects=True, vmem_limit_bytes=16 << 20
         ),
     )(lengths, dq, dk, dv, hidden, down_query, up_query, down_value, up_value)
 

time: 235 us -> 166 us (0.71)
  Pallas kernels: 219 us -> 160 us
  local copies, waits for them, and re-layouts: 13.4 us -> 5.37 us
    pallas_call x1, Pallas kernels: 88.7 us -> 65.2 us  [gather_heads(): pl.pallas_call(gather_kernel, name='gather_heads', out_shape=(head, head,...]
    pallas_call x1, Pallas kernels: 89.4 us -> 69.6 us  [adapters(): pl.pallas_call(adapter_kernel, name='return_and_adapters', out_shape=(gra...]
    pallas_call x1, Pallas kernels: 41.4 us -> 24.9 us  [attention_backward(): pl.pallas_call(attention_kernel, name='attention_backward', out_shape=(he...]
    unnamed x33 -> x19, local copies, waits for them, and re-layouts: 13.4 us -> 5.37 us
where the time goes in v2:
time: 166 us
  Pallas kernels  160 us (96%)
  local copies, waits for them, and re-layouts  5.37 us (3%)
    pallas_call x1, Pallas kernels, adapters(): pl.pallas_call(adapter_kernel, name='return_and_adapters', out_shape=(gra...  69.6 us
    pallas_call x1, Pallas kernels, gather_heads(): pl.pallas_call(gather_kernel, name='gather_heads', out_shape=(head, head,...  65.2 us
    pallas_call x1, Pallas kernels, attention_backward(): pl.pallas_call(attention_kernel, name='attention_backward', out_shape=(he...  24.9 us
    unnamed x19, local copies, waits for them, and re-layouts  5.37 us

profile of v2, /device:TPU:1, one launch (start us, length us, event | category | flops | bytes accessed | tf_op | source)
XLA Modules:
  0.0 165.8 jit_solution(18225660023808010159)
XLA Ops:
  0.6 0.0 copy-start.5
  0.6 65.2 %gather_heads.1 = (bf16[4096,128]{1,0:T(8,128)(2,1)S(1)}, bf16[4096,128]{1,0:T(8,128)(2,1)S(1)}, bf16[4096,128]{1,0:T(8,128)(2,1)S(1)}, bf16[4096,128]{1,0:T(8,128)(2,1)S(1)}, f32[32,1,128]{2,1,0:T(1,128)S(1)}) custom-call(bf16[128,4096]{1,0:T(8,128)(2,1)} %q_ref.1, bf16[128,4096]{1,0:T(8,128)(2,1)} %k_ref.1, bf16[128,4096]{1,0:T(8,128)(2,1)} %v_ref.1, ...), custom_call_target="tpu_custom_call" | custom-call | tf_op jit(solution)/shard_map/gather_heads/pallas_call | solution.py:149
  65.8 0.0 copy-done.5
  65.8 0.0 copy-start
  65.8 0.0 copy-start.1
  65.9 0.0 copy-start.2
  65.9 0.0 copy-start.3
  65.9 0.0 copy-start.4
  65.9 24.9 %attention_backward.1 = (bf16[4096,128]{1,0:T(8,128)(2,1)S(1)}, bf16[4096,128]{1,0:T(8,128)(2,1)S(1)}, bf16[4096,128]{1,0:T(8,128)(2,1)S(1)}) custom-call(s32[1,4]{1,0:T(1,128)S(1)} %copy-done.5, bf16[4096,128]{1,0:T(8,128)(2,1)S(1)} %get-tuple-element.15.q_ref, bf16[4096,128]{1,0:T(8,128)(2,1)S(1)} %get-tuple-element.16.k_ref, ...), custom_call_target="tpu_custom_call" | custom-call | tf_op jit(solution)/shard_map/attention_backward/pallas_call | solution.py:259
  90.8 0.0 copy-done
  90.8 0.0 copy-done.1
  90.8 0.0 copy-done.2
  90.8 0.0 copy-done.3
  90.8 0.0 copy-done.4
  90.8 69.6 %return_and_adapters.1 = (bf16[128,4096]{1,0:T(8,128)(2,1)S(1)}, bf16[128,4096]{1,0:T(8,128)(2,1)S(1)}, bf16[128,4096]{1,0:T(8,128)(2,1)S(1)}, f32[8,640]{1,0:T(...) custom-call(s32[1,4]{1,0:T(1,128)S(1)} %copy-done.5, ...), custom_call_target="tpu_custom_call" | custom-call | tf_op jit(solution)/shard_map/return_and_adapters/pallas_call | solution.py:513
  160.4 1.0 copy.25
  161.4 1.0 copy.26
  162.4 1.0 copy.27
  163.3 0.6 copy.28
  163.9 0.6 copy.29
  164.6 0.6 copy.30
  165.2 0.6 copy.31
Async XLA Ops:
  0.6 65.2 %copy-start.5 = (s32[1,4]{1,0:T(1,128)S(1)}, s32[1,4]{1,0:T(1,128)}, u32[]{:S(2)}) copy-start(s32[1,4]{1,0:T(1,128)} %len_ref.3) | copy-start | bytes 52
  65.8 24.9 %copy-start = (bf16[128,5120]{1,0:T(8,128)(2,1)S(1)}, bf16[128,5120]{1,0:T(8,128)(2,1)}, u32[]{:S(2)}) copy-start(bf16[128,5120]{1,0:T(8,128)(2,1)} %hid_ref.1) | copy-start | bytes 3932164
  65.8 24.9 %copy-start.1 = (bf16[8,5120]{1,0:T(8,128)(2,1)S(1)}, bf16[8,5120]{1,0:T(8,128)(2,1)}, u32[]{:S(2)}) copy-start(bf16[8,5120]{1,0:T(8,128)(2,1)} %downq.1) | copy-start | bytes 245764
  65.9 24.9 %copy-start.2 = (bf16[8,5120]{1,0:T(8,128)(2,1)S(1)}, bf16[8,5120]{1,0:T(8,128)(2,1)}, u32[]{:S(2)}) copy-start(bf16[8,5120]{1,0:T(8,128)(2,1)} %downv.1) | copy-start | bytes 245764
  65.9 24.9 %copy-start.3 = (bf16[8,4096]{1,0:T(8,128)(2,1)S(1)}, bf16[8,4096]{1,0:T(8,128)(2,1)}, u32[]{:S(2)}) copy-start(bf16[8,4096]{1,0:T(8,128)(2,1)} %upq.1) | copy-start | bytes 196612
  65.9 24.9 %copy-start.4 = (bf16[8,4096]{1,0:T(8,128)(2,1)S(1)}, bf16[8,4096]{1,0:T(8,128)(2,1)}, u32[]{:S(2)}) copy-start(bf16[8,4096]{1,0:T(8,128)(2,1)} %upv.1) | copy-start | bytes 196612

commit v3 on v2

v3 whole, which is shorter than its diff:
```python
import math

import jax
import jax.numpy as jnp
from jax import lax
from jax.experimental import pallas as pl
from jax.experimental.pallas import tpu as pltpu
from jax.sharding import PartitionSpec as P

H = 32
HD = 128
RANK = 8
ADAPTER_SCALE = 2.0
BQ = 512
BK = 512
GATHER_MIB = 48
LONGEST = 2048
SCALING = 1.0 / math.sqrt(HD)
TO_LOG2 = SCALING * math.log2(math.e)
MESH = pl.DeviceIdType.MESH
NT = (((1,), (1,)), ((), ()))
F32 = jnp.float32
BF16 = jnp.bfloat16


def nt_dot(a, b):
    return lax.dot_general(a, b, NT, preferred_element_type=F32)


def starts_of(len_ref):
    first = len_ref[0, 0]
    second = first + len_ref[0, 1]
    third = second + len_ref[0, 2]
    return first, second, third


def begin_of(positions, starts):
    found = jnp.zeros_like(positions)
    for start in starts:
        found = jnp.where(positions >= start, start, found)
    return found


def partner(me, step):
    chip = lax.rem(lax.rem(step, 16) * 7, 16)
    x = lax.rem(lax.div(me, 8) + lax.div(chip, 4), 4)
    y = lax.rem(lax.div(me, 2) + lax.rem(chip, 4), 4)
    return x * 8 + y * 2 + lax.rem(me + lax.div(step, 16), 2)


def partners(me):
    xs = [lax.rem(lax.div(me, 8) + d, 4) * 8 for d in range(4)]
    ys = [lax.rem(lax.div(me, 2) + d, 4) * 2 for d in range(4)]
    cores = [lax.rem(me + d, 2) for d in range(2)]
    chips = [step % 16 * 7 % 16 for step in range(32)]
    return [xs[chips[step] // 4] + ys[chips[step] % 4] + cores[step // 16] for step in range(32)]


def sender_of(me, step):
    chip = lax.rem(lax.rem(step, 16) * 7, 16)
    x = lax.rem(lax.div(me, 8) + 4 - lax.div(chip, 4), 4)
    y = lax.rem(lax.div(me, 2) + 4 - lax.rem(chip, 4), 4)
    return x * 8 + y * 2 + lax.rem(me + lax.div(step, 16), 2)


def gather_kernel(
    len_ref, q_ref, k_ref, v_ref, g_ref, o_ref, hid_ref, downq, downv,
    hq, hk, hv, hg, hd, hlow, lse, kt, table_ref,
    g_buf, o_buf, hid, wq, wv, d_buf, low, table, stat, send, recv, local, load,
):
    members = 32
    me = lax.axis_index("seq")
    rows = q_ref.shape[0]
    others = partners(me)
    barrier = pltpu.get_barrier_semaphore()
    for step in range(1, members):
        pl.semaphore_signal(barrier, inc=1, device_id={"seq": others[step]}, device_id_type=MESH)
    loads = [
        pltpu.make_async_copy(src, dst, load.at[index])
        for index, (src, dst) in enumerate(
            ((g_ref, g_buf), (o_ref, o_buf), (hid_ref, hid), (downq, wq), (downv, wv))
        )
    ]
    for copy in loads:
        copy.start()
    pairs = ((q_ref, hq), (k_ref, hk), (v_ref, hv), (g_ref, hg))
    my_rows = pl.ds(pl.multiple_of(me * rows, rows), rows)

    def columns(member):
        return pl.ds(pl.multiple_of(member * HD, HD), HD)

    own = [
        pltpu.make_async_copy(src.at[:, columns(me)], dst.at[my_rows, :], local.at[index])
        for index, (src, dst) in enumerate(pairs)
    ]
    for copy in own:
        copy.start()
    pl.semaphore_wait(barrier, members - 1)

    def copies(step, other, indices):
        moves = [(src.at[:, columns(other)], dst.at[my_rows, :]) for src, dst in pairs]
        moves.append((d_buf.at[other], hd.at[me]))
        moves.append((low, hlow.at[:, columns(me)]))
        return [
            pltpu.make_async_remote_copy(
                src_ref=src,
                dst_ref=dst,
                send_sem=send.at[index, step],
                recv_sem=recv.at[index, step],
                device_id={"seq": other},
                device_id_type=MESH,
            )
            for index, (src, dst) in enumerate(moves)
            if index in indices
        ]

    def start(indices):
        for step in range(1, members):
            for copy in copies(step, others[step], indices):
                copy.start()

    start((0, 1))
    for copy in loads:
        copy.wait()

    def delta_of(head, _):
        cols = columns(head)
        product = g_buf[:, cols].astype(F32) * o_buf[:, cols].astype(F32)
        d_buf[head] = jnp.sum(product.T, axis=0, keepdims=True)
        return 0

    lax.fori_loop(0, H, delta_of, 0)
    low[0:8, :] = nt_dot(wq[...], hid[...]).astype(BF16)
    low[8:16, :] = nt_dot(wv[...], hid[...]).astype(BF16)
    own_small = [
        pltpu.make_async_copy(d_buf.at[me], hd.at[me], local.at[4]),
        pltpu.make_async_copy(low, hlow.at[:, columns(me)], local.at[5]),
    ]
    for copy in own_small:
        copy.start()

    start((4, 5))
    start((2, 3))

    starts = starts_of(len_ref)
    lane = lax.broadcasted_iota(jnp.int32, (rows, HD), 1)
    pair = jnp.where(lane >= HD // 2, lane - HD // 2, lane).astype(F32)
    inverse = jnp.exp(-(pair * (2.0 / HD)) * math.log(10000.0))

    def angles(block, _):
        at = pl.multiple_of(block * rows, rows)
        token = at + lax.broadcasted_iota(jnp.int32, (rows, HD), 0)
        angle = (token - begin_of(token, starts)).astype(F32) * inverse
        table[pl.ds(at, rows), :] = jnp.where(lane >= HD // 2, jnp.sin(angle), jnp.cos(angle))
        return 0

    lax.fori_loop(0, members, angles, 0)
    store = pltpu.make_async_copy(table, table_ref, load.at[5])
    store.start()
    for copy in own + own_small:
        copy.wait()

    def arrived(step, _):
        for copy in copies(step, partner(me, step), (0, 1)):
            copy.wait_recv()
        return 0

    lax.fori_loop(1, members, arrived, 0)
    total = hq.shape[0]

    def turn(block, _):
        at = pl.multiple_of(block * 256, 256)
        kt[:, pl.ds(at, 256)] = hk[pl.ds(at, 256), :].T
        return 0

    lax.fori_loop(0, total // 256, turn, 0)

    def statistics(query_block, _):
        q0 = pl.multiple_of(query_block * BQ, BQ)
        q_rows = hq[pl.ds(q0, BQ), :]
        query_at = q0 + lax.broadcasted_iota(jnp.int32, (1, BQ), 1)
        query_begin = begin_of(query_at, starts)
        stat[0] = jnp.full((8, BQ), -1e30, F32)
        stat[1] = jnp.zeros((8, BQ), F32)

        def block(k0, diagonal):
            key_at = k0 + lax.broadcasted_iota(jnp.int32, (BQ, BQ), 0)
            allowed = key_at >= query_begin
            if diagonal:
                allowed = jnp.logical_and(allowed, key_at <= query_at)
            s = jnp.where(allowed, nt_dot(hk[pl.ds(k0, BQ), :], q_rows), -1e30)
            s = s.reshape(BQ // 8, 8, BQ)
            old = stat[0]
            new = jnp.maximum(old, jnp.max(s, axis=0))
            stat[0] = new
            stat[1] = stat[1] * jnp.exp2((old - new) * TO_LOG2) + jnp.sum(jnp.exp2((s - new[None]) * TO_LOG2), axis=0)

        def earlier(key_block, _):
            block(pl.multiple_of(key_block * BQ, BQ), False)
            return 0

        lax.fori_loop(jnp.maximum(query_block - LONGEST // BQ, 0), query_block, earlier, 0)
        block(q0, True)
        top = jnp.max(stat[0], axis=0, keepdims=True)
        weight = jnp.sum(stat[1] * jnp.exp2((stat[0] - top) * TO_LOG2), axis=0, keepdims=True)
        lse[query_block] = top * TO_LOG2 + jnp.log2(weight)
        return 0

    lax.fori_loop(0, total // BQ, statistics, 0)

    def finish(step, _):
        for copy in copies(step, partner(me, step), (0, 1)):
            copy.wait_send()
        for copy in copies(step, partner(me, step), (2, 3, 4, 5)):
            copy.wait()
        return 0

    lax.fori_loop(1, members, finish, 0)
    store.wait()


def gather_heads(lengths, queries, key_states, value_states, grad_out, attention_out, hidden, down_query, down_value):
    rows, width = queries.shape
    model = hidden.shape[1]
    hbm = pl.BlockSpec(memory_space=pltpu.HBM)
    vmem = pl.BlockSpec(memory_space=pltpu.VMEM)
    total = rows * 32
    head = jax.ShapeDtypeStruct((total, HD), BF16)
    return pl.pallas_call(
        gather_kernel,
        name="gather_heads",
        out_shape=(
            head, head, head, head,
            jax.ShapeDtypeStruct((32, 1, rows), F32),
            jax.ShapeDtypeStruct((2 * RANK, total), BF16),
            jax.ShapeDtypeStruct((total // BQ, 1, BQ), F32),
            jax.ShapeDtypeStruct((HD, total), BF16),
            jax.ShapeDtypeStruct((total, HD), F32),
        ),
        in_specs=[pl.BlockSpec(memory_space=pltpu.SMEM)] + [hbm] * 8,
        out_specs=[vmem] * 8 + [hbm],
        scratch_shapes=[
            pltpu.VMEM((rows, width), BF16),
            pltpu.VMEM((rows, width), BF16),
            pltpu.VMEM((rows, model), BF16),
            pltpu.VMEM((RANK, model), BF16),
            pltpu.VMEM((RANK, model), BF16),
            pltpu.VMEM((H, 1, rows), F32),
            pltpu.VMEM((2 * RANK, rows), BF16),
            pltpu.VMEM((total, HD), F32),
            pltpu.VMEM((2, 8, BQ), F32),
            pltpu.SemaphoreType.DMA((6, 32)),
            pltpu.SemaphoreType.DMA((6, 32)),
            pltpu.SemaphoreType.DMA((6,)),
            pltpu.SemaphoreType.DMA((6,)),
        ],
        compiler_params=pltpu.CompilerParams(
            collective_id=0, has_side_effects=True, vmem_limit_bytes=GATHER_MIB << 20
        ),
    )(lengths, queries, key_states, value_states, grad_out, attention_out, hidden, down_query, down_value)


def attention_kernel(
    len_ref, q_ref, k_ref, v_ref, g_ref, d_ref, lse_ref, kt, dq_ref, dk_ref, dv_ref, dk_acc, dv_acc, dq_acc
):
    total = q_ref.shape[0]
    starts = starts_of(len_ref)
    dk_acc[...] = jnp.zeros_like(dk_acc)
    dv_acc[...] = jnp.zeros_like(dv_acc)

    def outer(query_block, _):
        q0 = pl.multiple_of(query_block * BQ, BQ)
        q_rows = q_ref[pl.ds(q0, BQ), :]
        g_rows = g_ref[pl.ds(q0, BQ), :]
        delta = jnp.concatenate([d_ref[query_block * (BQ // 128) + i] for i in range(BQ // 128)], axis=1)
        lse = lse_ref[query_block]
        query_at = q0 + lax.broadcasted_iota(jnp.int32, (1, BQ), 1)
        query_begin = begin_of(query_at, starts)
        low = begin_of(q0, starts)
        high = begin_of(q0 + (BQ - 1), starts)
        first = lax.div(low, BK)
        last = lax.div(q0 + (BQ - 1), BK) + 1
        dq_acc[...] = jnp.zeros_like(dq_acc)

        def pair(key_block, _):
            k0 = pl.multiple_of(key_block * BK, BK)
            rows = pl.ds(k0, BK)
            inside = jnp.logical_and(high <= k0, k0 + (BK - 1) <= q0)

            def spread(s):
                weight = jnp.exp2(s * TO_LOG2 - lse)
                p = weight.astype(BF16)
                ds = (weight * (nt_dot(v_ref[rows, :], g_rows) - delta)).astype(BF16)
                dv_acc[rows, :] += jnp.dot(p, g_rows, preferred_element_type=F32)
                dk_acc[rows, :] += jnp.dot(ds, q_rows, preferred_element_type=F32)
                dq_acc[...] += jnp.dot(kt[:, rows], ds, preferred_element_type=F32)

            @pl.when(inside)
            def _():
                spread(nt_dot(k_ref[rows, :], q_rows))

            @pl.when(jnp.logical_not(inside))
            def _():
                key_at = k0 + lax.broadcasted_iota(jnp.int32, (BK, BQ), 0)
                allowed = jnp.logical_and(key_at >= query_begin, key_at <= query_at)
                spread(jnp.where(allowed, nt_dot(k_ref[rows, :], q_rows), -1e30))

            return 0

        lax.fori_loop(first, last, pair, 0)
        dq_ref[pl.ds(q0, BQ), :] = (dq_acc[...] * SCALING).T.astype(BF16)
        return 0

    lax.fori_loop(0, total // BQ, outer, 0)
    dk_ref[...] = (dk_acc[...] * SCALING).astype(BF16)
    dv_ref[...] = dv_acc[...].astype(BF16)


def attention_backward(lengths, q, k, v, g, delta, lse, kt):
    total = q.shape[0]
    vmem = pl.BlockSpec(memory_space=pltpu.VMEM)
    head = jax.ShapeDtypeStruct((total, HD), BF16)
    return pl.pallas_call(
        attention_kernel,
        name="attention_backward",
        out_shape=(head, head, head),
        in_specs=[pl.BlockSpec(memory_space=pltpu.SMEM)] + [vmem] * 7,
        out_specs=[vmem] * 3,
        scratch_shapes=[
            pltpu.VMEM((total, HD), F32),
            pltpu.VMEM((total, HD), F32),
            pltpu.VMEM((HD, BQ), F32),
        ],
        compiler_params=pltpu.CompilerParams(vmem_limit_bytes=20 << 20),
    )(lengths, q, k, v, g, delta, lse, kt)


def return_kernel(
    dq_ref, dk_ref, dv_ref, table, low, hid, upq, upv,
    gq_ref, gk_ref, gv_ref, done,
    back_out, back_in, part, z_in, up_part, up_in, tiles, r_in,
    send, recv, local, b_send, b_recv, z_send, z_recv, u_send, u_recv, r_send, r_recv, a_send, a_recv, c_send, c_recv,
):
    members, groups = 32, 8
    me = lax.axis_index("seq")
    dp = lax.axis_index("dp")
    rows = gq_ref.shape[0]
    total = dq_ref.shape[0]
    d_cols = hid.shape[1] // groups
    n_tiles = 2 * d_cols // 128
    chunk = 512
    barrier = pltpu.get_barrier_semaphore()

    def across(step):
        return lax.rem(dp + step, groups)

    others = partners(me)
    for step in range(1, members):
        pl.semaphore_signal(barrier, inc=1, device_id={"seq": others[step]}, device_id_type=MESH)
    for step in range(1, groups):
        pl.semaphore_signal(barrier, inc=1, device_id={"dp": across(step)}, device_id_type=MESH)
    pairs = ((dq_ref, gq_ref), (dv_ref, gv_ref), (dk_ref, gk_ref))
    my_cols = pl.ds(pl.multiple_of(me * HD, HD), HD)

    def rows_of(member):
        return pl.ds(pl.multiple_of(member * rows, rows), rows)

    own = [
        pltpu.make_async_copy(src.at[rows_of(me), :], dst.at[:, my_cols], local.at[index])
        for index, (src, dst) in enumerate(pairs)
    ]
    for copy in own:
        copy.start()
    pl.semaphore_wait(barrier, members - 1 + groups - 1)

    def to_member(src, dst, send_sem, recv_sem, other):
        return pltpu.make_async_remote_copy(
            src_ref=src, dst_ref=dst, send_sem=send_sem, recv_sem=recv_sem,
            device_id={"seq": other}, device_id_type=MESH,
        )

    def to_group(src, dst, send_sem, recv_sem, other):
        return pltpu.make_async_remote_copy(
            src_ref=src, dst_ref=dst, send_sem=send_sem, recv_sem=recv_sem,
            device_id={"dp": other}, device_id_type=MESH,
        )

    def bulk(index, step, other):
        src, dst = pairs[index]
        return to_member(
            src.at[rows_of(other), :], dst.at[:, my_cols], send.at[index, step], recv.at[index, step], other
        )

    def start_bulk(index):
        for step in range(1, members):
            bulk(index, step, others[step]).start()

    start_bulk(0)

    up_q = upq[:, my_cols]
    up_v = upv[:, my_cols]

    def share(block, sums):
        sum_q, sum_v = sums
        at = pl.multiple_of(block * chunk, chunk)
        here = pl.ds(at, chunk)
        wave = table[here, :]
        other_half = pltpu.roll(wave, HD // 2, 1)
        first = lax.broadcasted_iota(jnp.int32, (chunk, HD), 1) < HD // 2
        cosine = jnp.where(first, wave, other_half)
        sine = jnp.where(first, other_half, -wave)
        x = dq_ref[here, :].astype(F32)
        pre = (x * cosine + pltpu.roll(x, HD // 2, 1) * sine).astype(BF16)
        value = dv_ref[here, :]
        back_q = nt_dot(up_q, pre)
        back_v = nt_dot(up_v, value)
        for piece in range(chunk // rows):
            cols = slice(piece * rows, (piece + 1) * rows)
            back_out[block * (chunk // rows) + piece, 0:8, :] = back_q[:, cols]
            back_out[block * (chunk // rows) + piece, 8:16, :] = back_v[:, cols]
        low_q = low[0:8, here]
        low_v = low[8:16, here]
        return (
            sum_q + jnp.dot(low_q, pre, preferred_element_type=F32),
            sum_v + jnp.dot(low_v, value, preferred_element_type=F32),
        )

    zero = jnp.zeros((8, HD), F32)
    sum_q, sum_v = lax.fori_loop(0, total // chunk, share, (zero, zero))
    up_part[0] = sum_q
    up_part[1] = sum_v

    def back(step, other):
        return to_member(back_out.at[other], back_in.at[step], b_send.at[step], b_recv.at[step], other)

    for step in range(1, members):
        back(step, others[step]).start()
    owner = lax.div(me, members // groups)
    up_move = to_group(up_part, up_in.at[dp], u_send.at[dp], u_recv.at[dp], owner)

    @pl.when(owner != dp)
    def _():
        up_move.start()

    start_bulk(1)

    def add_back(step, summed):
        back(step, partner(me, step)).wait_recv()
        return summed + back_in[step]

    back_low = lax.fori_loop(1, members, add_back, back_out[me]).astype(BF16)
    for group in range(groups):
        part[group] = jnp.dot(back_low, hid[:, group * d_cols:(group + 1) * d_cols], preferred_element_type=F32)

    def exchange(step):
        other = across(step)
        return to_group(part.at[other], z_in.at[step], z_send.at[step], z_recv.at[step], other)

    for step in range(1, groups):
        exchange(step).start()
    start_bulk(2)

    def place_of(member):
        return pl.ds(n_tiles + 2 * lax.rem(member, members // groups), 2)

    def spread_up(step, other):
        mine = done.at[place_of(me)]
        return to_member(mine, mine, c_send.at[step], c_recv.at[step], other)

    def collect_up(step):
        theirs = done.at[place_of(sender_of(me, step))]
        return to_member(theirs, theirs, c_send.at[step], c_recv.at[step], partner(me, step))

    @pl.when(owner == dp)
    def _():
        summed = up_part[...]
        for step in range(1, groups):
            source = across(step)
            to_group(up_part, up_in.at[source], u_send.at[source], u_recv.at[source], source).wait_recv()
            summed = summed + up_in[source]
        done[place_of(me)] = summed * ADAPTER_SCALE

        for step in range(1, members):
            spread_up(step, others[step]).start()

    down = part[dp]
    for step in range(1, groups):
        exchange(step).wait()
        down = down + z_in[step]
    for tile in range(n_tiles):
        column, half = tile // 2, tile % 2
        tiles[tile] = down[half * 8:half * 8 + 8, column * 128:(column + 1) * 128]

    def scatter(step, other):
        return to_member(
            tiles.at[lax.rem(other, n_tiles)], r_in.at[step], r_send.at[step], r_recv.at[step], other
        )

    def spread(step, other):
        mine = done.at[lax.rem(me, n_tiles)]
        return to_member(mine, mine, a_send.at[step], a_recv.at[step], other)

    def collect(step):
        sender = sender_of(me, step)
        theirs = done.at[lax.rem(sender, n_tiles)]
        return sender, to_member(theirs, theirs, a_send.at[step], a_recv.at[step], partner(me, step))

    for step in range(1, members):
        @pl.when(others[step] < n_tiles)
        def _(step=step):
            scatter(step, others[step]).start()

    @pl.when(me < n_tiles)
    def _():
        def add_tile(step, summed):
            scatter(step, partner(me, step)).wait_recv()
            return summed + r_in[step]

        done[me] = lax.fori_loop(1, members, add_tile, tiles[me]) * ADAPTER_SCALE

        for step in range(1, members):
            spread(step, others[step]).start()

    def finish(step, _):
        for index in range(3):
            bulk(index, step, partner(me, step)).wait()
        back(step, partner(me, step)).wait_send()
        other = partner(me, step)

        @pl.when(other < n_tiles)
        def _():
            scatter(step, other).wait_send()

        @pl.when(me < n_tiles)
        def _():
            spread(step, other).wait_send()

        @pl.when(owner == dp)
        def _():
            spread_up(step, other).wait_send()

        sender, piece = collect(step)

        @pl.when(sender < n_tiles)
        def _():
            piece.wait_recv()

        @pl.when(lax.div(sender, members // groups) == dp)
        def _():
            collect_up(step).wait_recv()

        return 0

    lax.fori_loop(1, members, finish, 0)

    @pl.when(owner != dp)
    def _():
        up_move.wait_send()

    for copy in own:
        copy.wait()


def return_heads(dq, dk, dv, table, low, hidden, up_query, up_value):
    rows, model = hidden.shape
    total = dq.shape[0]
    width = up_query.shape[1]
    vmem = pl.BlockSpec(memory_space=pltpu.VMEM)
    grad = jax.ShapeDtypeStruct((rows, width), BF16)
    d_cols = model // 8
    n_tiles = 2 * d_cols // 128
    all_tiles = n_tiles + 2 * (width // 8) // 128
    dma = pltpu.SemaphoreType.DMA
    return pl.pallas_call(
        return_kernel,
        name="return_heads",
        out_shape=(grad, grad, grad, jax.ShapeDtypeStruct((all_tiles, 8, 128), F32)),
        in_specs=[vmem] * 8,
        out_specs=[vmem] * 4,
        scratch_shapes=[
            pltpu.VMEM((32, 2 * RANK, rows), F32),
            pltpu.VMEM((32, 2 * RANK, rows), F32),
            pltpu.VMEM((8, 2 * RANK, d_cols), F32),
            pltpu.VMEM((8, 2 * RANK, d_cols), F32),
            pltpu.VMEM((2, RANK, HD), F32),
            pltpu.VMEM((8, 2, RANK, HD), F32),
            pltpu.VMEM((n_tiles, 8, 128), F32),
            pltpu.VMEM((32, 8, 128), F32),
            dma((3, 32)), dma((3, 32)), dma((3,)),
            dma((32,)), dma((32,)),
            dma((8,)), dma((8,)),
            dma((8,)), dma((8,)),
            dma((32,)), dma((32,)),
            dma((32,)), dma((32,)),
            dma((32,)), dma((32,)),
        ],
        compiler_params=pltpu.CompilerParams(
            collective_id=1, has_side_effects=True, vmem_limit_bytes=16 << 20
        ),
    )(dq, dk, dv, table, low, hidden, up_query, up_value)


def finish_kernel(gq, gk, gv, done, oq, ok, ov, qd, qu, vd, vu, sems):
    copies = [
        pltpu.make_async_copy(src, dst, sems.at[index])
        for index, (src, dst) in enumerate(((gq, oq), (gk, ok), (gv, ov)))
    ]
    for copy in copies:
        copy.start()
    d_tiles = qd.shape[1] // 128
    for column in range(d_tiles):
        cols = slice(column * 128, (column + 1) * 128)
        qd[:, cols] = done[2 * column]
        vd[:, cols] = done[2 * column + 1]
    for column in range(qu.shape[1] // 128):
        cols = slice(column * 128, (column + 1) * 128)
        qu[:, cols] = done[2 * (d_tiles + column)]
        vu[:, cols] = done[2 * (d_tiles + column) + 1]
    for copy in copies:
        copy.wait()


def write_results(gq, gk, gv, done, model):
    rows, width = gq.shape
    vmem = pl.BlockSpec(memory_space=pltpu.VMEM)
    hbm = pl.BlockSpec(memory_space=pltpu.HBM)
    grad = jax.ShapeDtypeStruct((rows, width), BF16)
    down = jax.ShapeDtypeStruct((RANK, model // 8), F32)
    up = jax.ShapeDtypeStruct((RANK, width // 8), F32)
    return pl.pallas_call(
        finish_kernel,
        name="write_results",
        out_shape=(grad, grad, grad, down, up, down, up),
        in_specs=[vmem] * 4,
        out_specs=[hbm] * 3 + [vmem] * 4,
        scratch_shapes=[pltpu.SemaphoreType.DMA((3,))],
        compiler_params=pltpu.CompilerParams(vmem_limit_bytes=4 << 20),
    )(gq, gk, gv, done)


def shards(
    hidden,
    queries,
    key_states,
    value_states,
    attention_out,
    grad_out,
    lengths,
    down_query,
    up_query,
    down_value,
    up_value,
):
    q, k, v, g, delta, low, lse, kt, table = gather_heads(
        lengths, queries, key_states, value_states, grad_out, attention_out, hidden, down_query, down_value
    )
    dq, dk, dv = attention_backward(lengths, q, k, v, g, delta, lse, kt)
    gq, gk, gv, done = return_heads(dq, dk, dv, table, low, hidden, up_query, up_value)
    return write_results(gq, gk, gv, done, hidden.shape[1])


def solution(mesh):
    tokens = P(("dp", "seq"), None)
    return jax.shard_map(
        shards,
        mesh=mesh,
        in_specs=(tokens,) * 6 + (P("dp", None), P(), P(), P(), P()),
        out_specs=(tokens,) * 3 + (P(None, "dp"),) * 4,
        check_vma=False,
    )
```

time: 166 us -> 145 us (0.87)
  Pallas kernels: 160 us -> 142 us
  local copies, waits for them, and re-layouts: 5.37 us -> 2.44 us
    pallas_call x1 -> x2, Pallas kernels: 69.6 us -> 62.4 us  [the longest x1 60.1 us: return_heads(): pl.pallas_call(return_kernel, name='return_heads', out_shape=(grad, grad,...]
    pallas_call x1, Pallas kernels: 24.9 us -> 18.7 us  [attention_backward(): pl.pallas_call(attention_kernel, name='attention_backward', out_shape=(he...]
    pallas_call x1, Pallas kernels: 65.2 us -> 60.7 us  [gather_heads(): pl.pallas_call(gather_kernel, name='gather_heads', out_shape=(head, head,...]
    unnamed x19 -> x14, local copies, waits for them, and re-layouts: 5.37 us -> 2.44 us
where the time goes in v3:
time: 145 us
  Pallas kernels  142 us (98%)
  local copies, waits for them, and re-layouts  2.44 us (2%)
    pallas_call x1, Pallas kernels, gather_heads(): pl.pallas_call(gather_kernel, name='gather_heads', out_shape=(head, head,...  60.7 us
    pallas_call x1, Pallas kernels, return_heads(): pl.pallas_call(return_kernel, name='return_heads', out_shape=(grad, grad,...  60.1 us
    pallas_call x1, Pallas kernels, attention_backward(): pl.pallas_call(attention_kernel, name='attention_backward', out_shape=(he...  18.7 us

profile of v3, /device:TPU:1, one launch (start us, length us, event | category | flops | bytes accessed | tf_op | source)
XLA Modules:
  0.0 144.9 jit_solution(11800742102711549467)
XLA Ops:
  0.6 0.0 copy-start.2
  0.6 0.9 copy-done.2
  1.5 0.0 copy-start.3
  1.5 0.9 copy-done.3
  2.4 0.0 copy-start.6
  2.4 0.7 copy-done.6
  3.1 60.7 %gather_heads.1 = (bf16[4096,128]{1,0:T(8,128)(2,1)S(1)}, bf16[4096,128]{1,0:T(8,128)(2,1)S(1)}, bf16[4096,128]{1,0:T(8,128)(2,1)S(1)}, bf16[4096,128]{1,0:T(8,1...) custom-call(s32[1,4]{1,0:T(1,128)S(1)} %copy-done.6, ...), custom_call_target="tpu_custom_call" | custom-call | tf_op jit(solution)/shard_map/gather_heads/pallas_call | solution.py:229
  63.8 0.0 copy-start
  63.8 0.0 copy-start.1
  63.8 0.0 copy-start.4
  63.8 0.0 copy-start.5
  63.8 18.7 %attention_backward.1 = (bf16[4096,128]{1,0:T(8,128)(2,1)S(1)}, bf16[4096,128]{1,0:T(8,128)(2,1)S(1)}, bf16[4096,128]{1,0:T(8,128)(2,1)S(1)}) custom-call(s32[1,4]{1,0:T(1,128)S(1)} %copy-done.6, bf16[4096,128]{1,0:T(8,128)(2,1)S(1)} %get-tuple-element.23.q_ref, bf16[4096,128]{1,0:T(8,128)(2,1)S(1)} %get-tuple-element.24.k_ref, ...), custom_call_target="tpu_custom_call" | custom-call | tf_op jit(solution)/shard_map/attention_backward/pallas_call | solution.py:323
  82.5 0.0 copy-done
  82.5 0.0 copy-done.1
  82.5 0.0 copy-done.4
  82.5 0.0 copy-done.5
  82.5 60.1 %return_heads.1 = (bf16[128,4096]{1,0:T(8,128)(2,1)S(1)}, bf16[128,4096]{1,0:T(8,128)(2,1)S(1)}, bf16[128,4096]{1,0:T(8,128)(2,1)S(1)}, f32[18,8,128]{2,1,0:T(8,128)S(1)}) custom-call(bf16[4096,128]{1,0:T(8,128)(2,1)S(1)} %get-tuple-element.30.dq_ref, bf16[4096,128]{1,0:T(8,128)(2,1)S(1)} %get-tuple-element.31.dk_ref, ...), custom_call_target="tpu_custom_call" | custom-call | tf_op jit(solution)/shard_map/return_heads/pallas_call | solution.py:574
  142.6 2.3 %write_results.1 = (bf16[128,4096]{1,0:T(8,128)(2,1)}, bf16[128,4096]{1,0:T(8,128)(2,1)}, bf16[128,4096]{1,0:T(8,128)(2,1)}, f32[8,640]{1,0:T(8,128)}, f32[8,512...) custom-call(bf16[128,4096]{1,0:T(8,128)(2,1)S(1)} %get-tuple-element.35.gq, ...), custom_call_target="tpu_custom_call" | custom-call | tf_op jit(solution)/shard_map/write_results/pallas_call | solution.py:630
Async XLA Ops:
  0.6 0.9 copy-start.2
  1.5 0.9 copy-start.3
  2.4 0.7 copy-start.6
  63.8 18.7 %copy-start = (bf16[128,5120]{1,0:T(8,128)(2,1)S(1)}, bf16[128,5120]{1,0:T(8,128)(2,1)}, u32[]{:S(2)}) copy-start(bf16[128,5120]{1,0:T(8,128)(2,1)} %hid.1) | copy-start | bytes 3932164
  63.8 18.7 %copy-start.1 = (f32[4096,128]{1,0:T(8,128)S(1)}, f32[4096,128]{1,0:T(8,128)}, u32[]{:S(2)}) copy-start(f32[4096,128]{1,0:T(8,128)} %get-tuple-element.33.table) | copy-start | bytes 6291460
  63.8 18.7 %copy-start.4 = (bf16[8,4096]{1,0:T(8,128)(2,1)S(1)}, bf16[8,4096]{1,0:T(8,128)(2,1)}, u32[]{:S(2)}) copy-start(bf16[8,4096]{1,0:T(8,128)(2,1)} %upq.1) | copy-start | bytes 196612
  63.8 18.7 %copy-start.5 = (bf16[8,4096]{1,0:T(8,128)(2,1)S(1)}, bf16[8,4096]{1,0:T(8,128)(2,1)}, u32[]{:S(2)}) copy-start(bf16[8,4096]{1,0:T(8,128)(2,1)} %upv.1) | copy-start | bytes 196612

commit v4 on v3

--- a/solution.py
+++ b/solution.py
@@ -391,11 +391,14 @@
             src.at[rows_of(other), :], dst.at[:, my_cols], send.at[index, step], recv.at[index, step], other
         )
 
-    def start_bulk(index):
-        for step in range(1, members):
+    near = range(1, members // 2)
+    far = range(members // 2, members)
+
+    def start_bulk(index, steps):
+        for step in steps:
             bulk(index, step, others[step]).start()
 
-    start_bulk(0)
+    start_bulk(0, near)
 
     up_q = upq[:, my_cols]
     up_v = upv[:, my_cols]
@@ -442,23 +445,28 @@
     def _():
         up_move.start()
 
-    start_bulk(1)
+    start_bulk(0, far)
 
     def add_back(step, summed):
         back(step, partner(me, step)).wait_recv()
         return summed + back_in[step]
 
     back_low = lax.fori_loop(1, members, add_back, back_out[me]).astype(BF16)
-    for group in range(groups):
-        part[group] = jnp.dot(back_low, hid[:, group * d_cols:(group + 1) * d_cols], preferred_element_type=F32)
+
+    def fill(group):
+        cols = pl.ds(pl.multiple_of(group * d_cols, 128), d_cols)
+        part[group] = jnp.dot(back_low, hid[:, cols], preferred_element_type=F32)
 
     def exchange(step):
         other = across(step)
         return to_group(part.at[other], z_in.at[step], z_send.at[step], z_recv.at[step], other)
 
     for step in range(1, groups):
+        fill(across(step))
         exchange(step).start()
-    start_bulk(2)
+    start_bulk(1, near)
+    start_bulk(1, far)
+    fill(dp)
 
     def place_of(member):
         return pl.ds(n_tiles + 2 * lax.rem(member, members // groups), 2)
@@ -510,6 +518,8 @@
         def _(step=step):
             scatter(step, others[step]).start()
 
+    start_bulk(2, near)
+
     @pl.when(me < n_tiles)
     def _():
         def add_tile(step, summed):
@@ -520,6 +530,8 @@
 
         for step in range(1, members):
             spread(step, others[step]).start()
+
+    start_bulk(2, far)
 
     def finish(step, _):
         for index in range(3):

time: 145 us -> 143 us (0.986)
  Pallas kernels: 142 us -> 139 us
    pallas_call x1, Pallas kernels: 60.1 us -> 57.7 us  [return_heads(): pl.pallas_call(return_kernel, name='return_heads', out_shape=(grad, grad,...]
where the time goes in v4:
time: 143 us
  Pallas kernels  139 us (97%)
  local copies, waits for them, and re-layouts  2.44 us (2%)
    pallas_call x1, Pallas kernels, gather_heads(): pl.pallas_call(gather_kernel, name='gather_heads', out_shape=(head, head,...  60.7 us
    pallas_call x1, Pallas kernels, return_heads(): pl.pallas_call(return_kernel, name='return_heads', out_shape=(grad, grad,...  57.7 us
    pallas_call x1, Pallas kernels, attention_backward(): pl.pallas_call(attention_kernel, name='attention_backward', out_shape=(he...  18.7 us

profile of v4, /device:TPU:1, one launch (start us, length us, event | category | flops | bytes accessed | tf_op | source)
XLA Modules:
  0.0 142.5 jit_solution(16249303400765723204)
XLA Ops:
  0.6 0.0 copy-start.2
  0.6 0.9 copy-done.2
  1.5 0.0 copy-start.3
  1.5 0.9 copy-done.3
  2.4 0.0 copy-start.6
  2.4 0.7 copy-done.6
  3.1 60.7 %gather_heads.1 = (bf16[4096,128]{1,0:T(8,128)(2,1)S(1)}, bf16[4096,128]{1,0:T(8,128)(2,1)S(1)}, bf16[4096,128]{1,0:T(8,128)(2,1)S(1)}, bf16[4096,128]{1,0:T(8,1...) custom-call(s32[1,4]{1,0:T(1,128)S(1)} %copy-done.6, ...), custom_call_target="tpu_custom_call" | custom-call | tf_op jit(solution)/shard_map/gather_heads/pallas_call | solution.py:229
  63.8 0.0 copy-start
  63.8 0.0 copy-start.1
  63.8 0.0 copy-start.4
  63.8 0.0 copy-start.5
  63.8 18.7 %attention_backward.1 = (bf16[4096,128]{1,0:T(8,128)(2,1)S(1)}, bf16[4096,128]{1,0:T(8,128)(2,1)S(1)}, bf16[4096,128]{1,0:T(8,128)(2,1)S(1)}) custom-call(s32[1,4]{1,0:T(1,128)S(1)} %copy-done.6, bf16[4096,128]{1,0:T(8,128)(2,1)S(1)} %get-tuple-element.23.q_ref, bf16[4096,128]{1,0:T(8,128)(2,1)S(1)} %get-tuple-element.24.k_ref, ...), custom_call_target="tpu_custom_call" | custom-call | tf_op jit(solution)/shard_map/attention_backward/pallas_call | solution.py:323
  82.5 0.0 copy-done
  82.5 0.0 copy-done.1
  82.5 0.0 copy-done.4
  82.5 0.0 copy-done.5
  82.5 57.7 %return_heads.1 = (bf16[128,4096]{1,0:T(8,128)(2,1)S(1)}, bf16[128,4096]{1,0:T(8,128)(2,1)S(1)}, bf16[128,4096]{1,0:T(8,128)(2,1)S(1)}, f32[18,8,128]{2,1,0:T(8,128)S(1)}) custom-call(bf16[4096,128]{1,0:T(8,128)(2,1)S(1)} %get-tuple-element.30.dq_ref, bf16[4096,128]{1,0:T(8,128)(2,1)S(1)} %get-tuple-element.31.dk_ref, ...), custom_call_target="tpu_custom_call" | custom-call | tf_op jit(solution)/shard_map/return_heads/pallas_call | solution.py:586
  140.2 2.3 %write_results.1 = (bf16[128,4096]{1,0:T(8,128)(2,1)}, bf16[128,4096]{1,0:T(8,128)(2,1)}, bf16[128,4096]{1,0:T(8,128)(2,1)}, f32[8,640]{1,0:T(8,128)}, f32[8,512...) custom-call(bf16[128,4096]{1,0:T(8,128)(2,1)S(1)} %get-tuple-element.35.gq, ...), custom_call_target="tpu_custom_call" | custom-call | tf_op jit(solution)/shard_map/write_results/pallas_call | solution.py:642
Async XLA Ops:
  0.6 0.9 copy-start.2
  1.5 0.9 copy-start.3
  2.4 0.7 copy-start.6
  63.8 18.7 %copy-start = (bf16[128,5120]{1,0:T(8,128)(2,1)S(1)}, bf16[128,5120]{1,0:T(8,128)(2,1)}, u32[]{:S(2)}) copy-start(bf16[128,5120]{1,0:T(8,128)(2,1)} %hid.1) | copy-start | bytes 3932164
  63.8 18.7 %copy-start.1 = (f32[4096,128]{1,0:T(8,128)S(1)}, f32[4096,128]{1,0:T(8,128)}, u32[]{:S(2)}) copy-start(f32[4096,128]{1,0:T(8,128)} %get-tuple-element.33.table) | copy-start | bytes 6291460
  63.8 18.7 %copy-start.4 = (bf16[8,4096]{1,0:T(8,128)(2,1)S(1)}, bf16[8,4096]{1,0:T(8,128)(2,1)}, u32[]{:S(2)}) copy-start(bf16[8,4096]{1,0:T(8,128)(2,1)} %upq.1) | copy-start | bytes 196612
  63.8 18.7 %copy-start.5 = (bf16[8,4096]{1,0:T(8,128)(2,1)S(1)}, bf16[8,4096]{1,0:T(8,128)(2,1)}, u32[]{:S(2)}) copy-start(bf16[8,4096]{1,0:T(8,128)(2,1)} %upv.1) | copy-start | bytes 196612

commit v5 on v4

--- a/solution.py
+++ b/solution.py
@@ -41,13 +41,6 @@
     return found
 
 
-def partner(me, step):
-    chip = lax.rem(lax.rem(step, 16) * 7, 16)
-    x = lax.rem(lax.div(me, 8) + lax.div(chip, 4), 4)
-    y = lax.rem(lax.div(me, 2) + lax.rem(chip, 4), 4)
-    return x * 8 + y * 2 + lax.rem(me + lax.div(step, 16), 2)
-
-
 def partners(me):
     xs = [lax.rem(lax.div(me, 8) + d, 4) * 8 for d in range(4)]
     ys = [lax.rem(lax.div(me, 2) + d, 4) * 2 for d in range(4)]
@@ -56,11 +49,11 @@
     return [xs[chips[step] // 4] + ys[chips[step] % 4] + cores[step // 16] for step in range(32)]
 
 
-def sender_of(me, step):
-    chip = lax.rem(lax.rem(step, 16) * 7, 16)
-    x = lax.rem(lax.div(me, 8) + 4 - lax.div(chip, 4), 4)
-    y = lax.rem(lax.div(me, 2) + 4 - lax.rem(chip, 4), 4)
-    return x * 8 + y * 2 + lax.rem(me + lax.div(step, 16), 2)
+def bytes_of(ref, send_sem, recv_sem, other):
+    return pltpu.make_async_remote_copy(
+        src_ref=ref, dst_ref=ref, send_sem=send_sem, recv_sem=recv_sem,
+        device_id={"seq": other}, device_id_type=MESH,
+    )
 
 
 def gather_kernel(
@@ -97,7 +90,7 @@
         copy.start()
     pl.semaphore_wait(barrier, members - 1)
 
-    def copies(step, other, indices):
+    def copies(other, indices):
         moves = [(src.at[:, columns(other)], dst.at[my_rows, :]) for src, dst in pairs]
         moves.append((d_buf.at[other], hd.at[me]))
         moves.append((low, hlow.at[:, columns(me)]))
@@ -105,8 +98,8 @@
             pltpu.make_async_remote_copy(
                 src_ref=src,
                 dst_ref=dst,
-                send_sem=send.at[index, step],
-                recv_sem=recv.at[index, step],
+                send_sem=send.at[index],
+                recv_sem=recv.at[index],
                 device_id={"seq": other},
                 device_id_type=MESH,
             )
@@ -116,7 +109,7 @@
 
     def start(indices):
         for step in range(1, members):
-            for copy in copies(step, others[step], indices):
+            for copy in copies(others[step], indices):
                 copy.start()
 
     start((0, 1))
@@ -160,12 +153,12 @@
     for copy in own + own_small:
         copy.wait()
 
-    def arrived(step, _):
-        for copy in copies(step, partner(me, step), (0, 1)):
-            copy.wait_recv()
-        return 0
-
-    lax.fori_loop(1, members, arrived, 0)
+    slots = members - 1
+    landed = [dst.at[pl.ds(0, slots * rows), :] for _, dst in pairs]
+    landed += [hd.at[pl.ds(0, slots)], hlow.at[:, pl.ds(0, slots * rows)]]
+    moved = [bytes_of(ref, send.at[index], recv.at[index], others[1]) for index, ref in enumerate(landed)]
+    moved[0].wait_recv()
+    moved[1].wait_recv()
     total = hq.shape[0]
 
     def turn(block, _):
@@ -208,14 +201,10 @@
 
     lax.fori_loop(0, total // BQ, statistics, 0)
 
-    def finish(step, _):
-        for copy in copies(step, partner(me, step), (0, 1)):
-            copy.wait_send()
-        for copy in copies(step, partner(me, step), (2, 3, 4, 5)):
-            copy.wait()
-        return 0
-
-    lax.fori_loop(1, members, finish, 0)
+    moved[0].wait_send()
+    moved[1].wait_send()
+    for copy in moved[2:]:
+        copy.wait()
     store.wait()
 
 
@@ -249,8 +238,8 @@
             pltpu.VMEM((2 * RANK, rows), BF16),
             pltpu.VMEM((total, HD), F32),
             pltpu.VMEM((2, 8, BQ), F32),
-            pltpu.SemaphoreType.DMA((6, 32)),
-            pltpu.SemaphoreType.DMA((6, 32)),
+            pltpu.SemaphoreType.DMA((6,)),
+            pltpu.SemaphoreType.DMA((6,)),
             pltpu.SemaphoreType.DMA((6,)),
             pltpu.SemaphoreType.DMA((6,)),
         ],
@@ -385,10 +374,10 @@
             device_id={"dp": other}, device_id_type=MESH,
         )
 
-    def bulk(index, step, other):
+    def bulk(index, other):
         src, dst = pairs[index]
         return to_member(
-            src.at[rows_of(other), :], dst.at[:, my_cols], send.at[index, step], recv.at[index, step], other
+            src.at[rows_of(other), :], dst.at[:, my_cols], send.at[index], recv.at[index], other
         )
 
     near = range(1, members // 2)
@@ -396,7 +385,7 @@
 
     def start_bulk(index, steps):
         for step in steps:
-            bulk(index, step, others[step]).start()
+            bulk(index, others[step]).start()
 
     start_bulk(0, near)
 
@@ -434,7 +423,7 @@
     up_part[1] = sum_v
 
     def back(step, other):
-        return to_member(back_out.at[other], back_in.at[step], b_send.at[step], b_recv.at[step], other)
+        return to_member(back_out.at[other], back_in.at[step - 1], b_send, b_recv, other)
 
     for step in range(1, members):
         back(step, others[step]).start()
@@ -447,11 +436,11 @@
 
     start_bulk(0, far)
 
-    def add_back(step, summed):
-        back(step, partner(me, step)).wait_recv()
-        return summed + back_in[step]
-
-    back_low = lax.fori_loop(1, members, add_back, back_out[me]).astype(BF16)
+    slots = members - 1
+    backs = bytes_of(back_in.at[pl.ds(0, slots)], b_send, b_recv, others[1])
+    backs.wait_recv()
+    back_low = jnp.sum(back_in[0:slots], axis=0) + back_out[me]
+    back_low = back_low.astype(BF16)
 
     def fill(group):
         cols = pl.ds(pl.multiple_of(group * d_cols, 128), d_cols)
@@ -473,11 +462,7 @@
 
     def spread_up(step, other):
         mine = done.at[place_of(me)]
-        return to_member(mine, mine, c_send.at[step], c_recv.at[step], other)
-
-    def collect_up(step):
-        theirs = done.at[place_of(sender_of(me, step))]
-        return to_member(theirs, theirs, c_send.at[step], c_recv.at[step], partner(me, step))
+        return to_member(mine, mine, c_send, c_recv, other)
 
     @pl.when(owner == dp)
     def _():
@@ -501,17 +486,12 @@
 
     def scatter(step, other):
         return to_member(
-            tiles.at[lax.rem(other, n_tiles)], r_in.at[step], r_send.at[step], r_recv.at[step], other
+            tiles.at[lax.rem(other, n_tiles)], r_in.at[step - 1], r_send, r_recv, other
         )
 
     def spread(step, other):
         mine = done.at[lax.rem(me, n_tiles)]
-        return to_member(mine, mine, a_send.at[step], a_recv.at[step], other)
-
-    def collect(step):
-        sender = sender_of(me, step)
-        theirs = done.at[lax.rem(sender, n_tiles)]
-        return sender, to_member(theirs, theirs, a_send.at[step], a_recv.at[step], partner(me, step))
+        return to_member(mine, mine, a_send, a_recv, other)
 
     for step in range(1, members):
         @pl.when(others[step] < n_tiles)
@@ -522,48 +502,39 @@
 
     @pl.when(me < n_tiles)
     def _():
-        def add_tile(step, summed):
-            scatter(step, partner(me, step)).wait_recv()
-            return summed + r_in[step]
-
-        done[me] = lax.fori_loop(1, members, add_tile, tiles[me]) * ADAPTER_SCALE
-
+        bytes_of(r_in, r_send, r_recv, others[1]).wait_recv()
+        done[me] = (tiles[me] + jnp.sum(r_in[...], axis=0)) * ADAPTER_SCALE
         for step in range(1, members):
             spread(step, others[step]).start()
 
     start_bulk(2, far)
 
-    def finish(step, _):
-        for index in range(3):
-            bulk(index, step, partner(me, step)).wait()
-        back(step, partner(me, step)).wait_send()
-        other = partner(me, step)
-
-        @pl.when(other < n_tiles)
-        def _():
-            scatter(step, other).wait_send()
-
-        @pl.when(me < n_tiles)
-        def _():
-            spread(step, other).wait_send()
-
-        @pl.when(owner == dp)
-        def _():
-            spread_up(step, other).wait_send()
-
-        sender, piece = collect(step)
-
-        @pl.when(sender < n_tiles)
-        def _():
-            piece.wait_recv()
-
-        @pl.when(lax.div(sender, members // groups) == dp)
-        def _():
-            collect_up(step).wait_recv()
-
-        return 0
-
-    lax.fori_loop(1, members, finish, 0)
+    backs.wait_send()
+
+    @pl.when(me < n_tiles)
+    def _():
+        bytes_of(tiles.at[pl.ds(0, n_tiles - 1)], r_send, r_recv, others[1]).wait_send()
+        bytes_of(r_in, a_send, a_recv, others[1]).wait_send()
+        bytes_of(tiles.at[pl.ds(0, n_tiles - 1)], a_send, a_recv, others[1]).wait_recv()
+
+    @pl.when(me >= n_tiles)
+    def _():
+        bytes_of(tiles, r_send, r_recv, others[1]).wait_send()
+        bytes_of(tiles, a_send, a_recv, others[1]).wait_recv()
+
+    per_group = members // groups
+
+    @pl.when(owner == dp)
+    def _():
+        bytes_of(back_in.at[pl.ds(0, slots)], c_send, c_recv, others[1]).wait_send()
+        bytes_of(up_in.at[pl.ds(0, per_group - 1)], c_send, c_recv, others[1]).wait_recv()
+
+    @pl.when(owner != dp)
+    def _():
+        bytes_of(up_in.at[pl.ds(0, per_group)], c_send, c_recv, others[1]).wait_recv()
+
+    for index, (_, dst) in enumerate(pairs):
+        bytes_of(dst.at[:, pl.ds(0, slots * HD)], send.at[index], recv.at[index], others[1]).wait()
 
     @pl.when(owner != dp)
     def _():
@@ -597,14 +568,14 @@
             pltpu.VMEM((2, RANK, HD), F32),
             pltpu.VMEM((8, 2, RANK, HD), F32),
             pltpu.VMEM((n_tiles, 8, 128), F32),
-            pltpu.VMEM((32, 8, 128), F32),
-            dma((3, 32)), dma((3, 32)), dma((3,)),
-            dma((32,)), dma((32,)),
+            pltpu.VMEM((31, 8, 128), F32),
+            dma((3,)), dma((3,)), dma((3,)),
+            dma, dma,
             dma((8,)), dma((8,)),
             dma((8,)), dma((8,)),
-            dma((32,)), dma((32,)),
-            dma((32,)), dma((32,)),
-            dma((32,)), dma((32,)),
+            dma, dma,
+            dma, dma,
+            dma, dma,
         ],
         compiler_params=pltpu.CompilerParams(
             collective_id=1, has_side_effects=True, vmem_limit_bytes=16 << 20

time: 143 us -> 135 us (0.944)
  Pallas kernels: 139 us -> 131 us
    pallas_call x1, Pallas kernels: 57.7 us -> 48.7 us  [return_heads(): pl.pallas_call(return_kernel, name='return_heads', out_shape=(grad, grad,...]
    pallas_call x1, Pallas kernels: 18.7 us -> 22.9 us  [attention_backward(): pl.pallas_call(attention_kernel, name='attention_backward', out_shape=(he...]
    pallas_call x1, Pallas kernels: 60.7 us -> 57.3 us  [gather_heads(): pl.pallas_call(gather_kernel, name='gather_heads', out_shape=(head, head,...]
where the time goes in v5:
time: 135 us
  Pallas kernels  131 us (97%)
  local copies, waits for them, and re-layouts  2.44 us (2%)
    pallas_call x1, Pallas kernels, gather_heads(): pl.pallas_call(gather_kernel, name='gather_heads', out_shape=(head, head,...  57.3 us
    pallas_call x1, Pallas kernels, return_heads(): pl.pallas_call(return_kernel, name='return_heads', out_shape=(grad, grad,...  48.7 us
    pallas_call x1, Pallas kernels, attention_backward(): pl.pallas_call(attention_kernel, name='attention_backward', out_shape=(he...  22.9 us

profile of v5, /device:TPU:1, one launch (start us, length us, event | category | flops | bytes accessed | tf_op | source)
XLA Modules:
  0.0 134.5 jit_solution(6011702499040612045)
XLA Ops:
  0.6 0.0 copy-start.2
  0.6 0.9 copy-done.2
  1.5 0.0 copy-start.3
  1.5 0.9 copy-done.3
  2.4 0.0 copy-start.6
  2.4 0.7 copy-done.6
  3.1 57.3 %gather_heads.1 = (bf16[4096,128]{1,0:T(8,128)(2,1)S(1)}, bf16[4096,128]{1,0:T(8,128)(2,1)S(1)}, bf16[4096,128]{1,0:T(8,128)(2,1)S(1)}, bf16[4096,128]{1,0:T(8,1...) custom-call(s32[1,4]{1,0:T(1,128)S(1)} %copy-done.6, ...), custom_call_target="tpu_custom_call" | custom-call | tf_op jit(solution)/shard_map/gather_heads/pallas_call | solution.py:218
  60.4 0.0 copy-start
  60.4 0.0 copy-start.1
  60.4 0.0 copy-start.4
  60.5 0.0 copy-start.5
  60.5 22.9 %attention_backward.1 = (bf16[4096,128]{1,0:T(8,128)(2,1)S(1)}, bf16[4096,128]{1,0:T(8,128)(2,1)S(1)}, bf16[4096,128]{1,0:T(8,128)(2,1)S(1)}) custom-call(s32[1,4]{1,0:T(1,128)S(1)} %copy-done.6, bf16[4096,128]{1,0:T(8,128)(2,1)S(1)} %get-tuple-element.23.q_ref, bf16[4096,128]{1,0:T(8,128)(2,1)S(1)} %get-tuple-element.24.k_ref, ...), custom_call_target="tpu_custom_call" | custom-call | tf_op jit(solution)/shard_map/attention_backward/pallas_call | solution.py:312
  83.4 0.0 copy-done
  83.4 0.0 copy-done.1
  83.4 0.0 copy-done.4
  83.4 0.0 copy-done.5
  83.5 48.7 %return_heads.1 = (bf16[128,4096]{1,0:T(8,128)(2,1)S(1)}, bf16[128,4096]{1,0:T(8,128)(2,1)S(1)}, bf16[128,4096]{1,0:T(8,128)(2,1)S(1)}, f32[18,8,128]{2,1,0:T(8,128)S(1)}) custom-call(bf16[4096,128]{1,0:T(8,128)(2,1)S(1)} %get-tuple-element.30.dq_ref, bf16[4096,128]{1,0:T(8,128)(2,1)S(1)} %get-tuple-element.31.dk_ref, ...), custom_call_target="tpu_custom_call" | custom-call | tf_op jit(solution)/shard_map/return_heads/pallas_call | solution.py:557
  132.2 2.3 %write_results.1 = (bf16[128,4096]{1,0:T(8,128)(2,1)}, bf16[128,4096]{1,0:T(8,128)(2,1)}, bf16[128,4096]{1,0:T(8,128)(2,1)}, f32[8,640]{1,0:T(8,128)}, f32[8,512...) custom-call(bf16[128,4096]{1,0:T(8,128)(2,1)S(1)} %get-tuple-element.35.gq, ...), custom_call_target="tpu_custom_call" | custom-call | tf_op jit(solution)/shard_map/write_results/pallas_call | solution.py:613
Async XLA Ops:
  0.6 0.9 copy-start.2
  1.5 0.9 copy-start.3
  2.4 0.7 copy-start.6
  60.4 23.0 %copy-start = (bf16[128,5120]{1,0:T(8,128)(2,1)S(1)}, bf16[128,5120]{1,0:T(8,128)(2,1)}, u32[]{:S(2)}) copy-start(bf16[128,5120]{1,0:T(8,128)(2,1)} %hid.1) | copy-start | bytes 3932164
  60.4 23.0 %copy-start.1 = (f32[4096,128]{1,0:T(8,128)S(1)}, f32[4096,128]{1,0:T(8,128)}, u32[]{:S(2)}) copy-start(f32[4096,128]{1,0:T(8,128)} %get-tuple-element.33.table) | copy-start | bytes 6291460
  60.4 23.0 %copy-start.4 = (bf16[8,4096]{1,0:T(8,128)(2,1)S(1)}, bf16[8,4096]{1,0:T(8,128)(2,1)}, u32[]{:S(2)}) copy-start(bf16[8,4096]{1,0:T(8,128)(2,1)} %upq.1) | copy-start | bytes 196612
  60.5 23.0 %copy-start.5 = (bf16[8,4096]{1,0:T(8,128)(2,1)S(1)}, bf16[8,4096]{1,0:T(8,128)(2,1)}, u32[]{:S(2)}) copy-start(bf16[8,4096]{1,0:T(8,128)(2,1)} %upv.1) | copy-start | bytes 196612

commit v6 on v5

--- a/solution.py
+++ b/solution.py
@@ -276,23 +276,36 @@
             rows = pl.ds(k0, BK)
             inside = jnp.logical_and(high <= k0, k0 + (BK - 1) <= q0)
 
-            def spread(s):
-                weight = jnp.exp2(s * TO_LOG2 - lse)
+            def spread(rows, skip, s):
+                weight = jnp.exp2(s * TO_LOG2 - lse[:, skip:])
                 p = weight.astype(BF16)
-                ds = (weight * (nt_dot(v_ref[rows, :], g_rows) - delta)).astype(BF16)
-                dv_acc[rows, :] += jnp.dot(p, g_rows, preferred_element_type=F32)
-                dk_acc[rows, :] += jnp.dot(ds, q_rows, preferred_element_type=F32)
-                dq_acc[...] += jnp.dot(kt[:, rows], ds, preferred_element_type=F32)
+                grad_p = nt_dot(v_ref[rows, :], g_rows[skip:, :])
+                ds = (weight * (grad_p - delta[:, skip:])).astype(BF16)
+                dv_acc[rows, :] += jnp.dot(p, g_rows[skip:, :], preferred_element_type=F32)
+                dk_acc[rows, :] += jnp.dot(ds, q_rows[skip:, :], preferred_element_type=F32)
+                dq_acc[:, skip:] += jnp.dot(kt[:, rows], ds, preferred_element_type=F32)
+
+            def masked(rows, key0, count, skip):
+                key_at = key0 + lax.broadcasted_iota(jnp.int32, (count, BQ - skip), 0)
+                allowed = jnp.logical_and(key_at >= query_begin[:, skip:], key_at <= query_at[:, skip:])
+                return jnp.where(allowed, nt_dot(k_ref[rows, :], q_rows[skip:, :]), -1e30)
+
+            diagonal = key_block == query_block
 
             @pl.when(inside)
             def _():
-                spread(nt_dot(k_ref[rows, :], q_rows))
-
-            @pl.when(jnp.logical_not(inside))
+                spread(rows, 0, nt_dot(k_ref[rows, :], q_rows))
+
+            @pl.when(jnp.logical_not(jnp.logical_or(inside, diagonal)))
             def _():
-                key_at = k0 + lax.broadcasted_iota(jnp.int32, (BK, BQ), 0)
-                allowed = jnp.logical_and(key_at >= query_begin, key_at <= query_at)
-                spread(jnp.where(allowed, nt_dot(k_ref[rows, :], q_rows), -1e30))
+                spread(rows, 0, masked(rows, k0, BK, 0))
+
+            @pl.when(diagonal)
+            def _():
+                for skip in (0, BQ // 2):
+                    at = pl.multiple_of(k0 + skip, BQ // 2)
+                    part = pl.ds(at, BQ // 2)
+                    spread(part, skip, masked(part, at, BQ // 2, skip))
 
             return 0
 

time: 135 us -> 137 us (1.015); the launches traced: 135 us -> 135 us
    pallas_call x1, Pallas kernels: 48.7 us -> 54.4 us  [return_heads(): pl.pallas_call(return_kernel, name='return_heads', out_shape=(grad, grad,...]
    pallas_call x1, Pallas kernels: 22.9 us -> 17.7 us  [attention_backward(): pl.pallas_call(attention_kernel, name='attention_backward', out_shape=(he...]
where the time goes in v6:
time: 137 us; the launch traced here: 135 us
  Pallas kernels  132 us (96%)
  local copies, waits for them, and re-layouts  2.44 us (2%)
    pallas_call x1, Pallas kernels, gather_heads(): pl.pallas_call(gather_kernel, name='gather_heads', out_shape=(head, head,...  57.3 us
    pallas_call x1, Pallas kernels, return_heads(): pl.pallas_call(return_kernel, name='return_heads', out_shape=(grad, grad,...  54.4 us
    pallas_call x1, Pallas kernels, attention_backward(): pl.pallas_call(attention_kernel, name='attention_backward', out_shape=(he...  17.7 us

profile of v6, /device:TPU:1, one launch (start us, length us, event | category | flops | bytes accessed | tf_op | source)
XLA Modules:
  0.0 134.9 jit_solution(7138428412934973647)
XLA Ops:
  0.6 0.0 copy-start.2
  0.6 0.9 copy-done.2
  1.5 0.0 copy-start.3
  1.5 0.9 copy-done.3
  2.4 0.0 copy-start.6
  2.4 0.7 copy-done.6
  3.1 57.3 %gather_heads.1 = (bf16[4096,128]{1,0:T(8,128)(2,1)S(1)}, bf16[4096,128]{1,0:T(8,128)(2,1)S(1)}, bf16[4096,128]{1,0:T(8,128)(2,1)S(1)}, bf16[4096,128]{1,0:T(8,1...) custom-call(s32[1,4]{1,0:T(1,128)S(1)} %copy-done.6, ...), custom_call_target="tpu_custom_call" | custom-call | tf_op jit(solution)/shard_map/gather_heads/pallas_call | solution.py:218
  60.4 0.0 copy-start
  60.4 0.0 copy-start.1
  60.4 0.0 copy-start.4
  60.5 0.0 copy-start.5
  60.5 17.7 %attention_backward.1 = (bf16[4096,128]{1,0:T(8,128)(2,1)S(1)}, bf16[4096,128]{1,0:T(8,128)(2,1)S(1)}, bf16[4096,128]{1,0:T(8,128)(2,1)S(1)}) custom-call(s32[1,4]{1,0:T(1,128)S(1)} %copy-done.6, bf16[4096,128]{1,0:T(8,128)(2,1)S(1)} %get-tuple-element.23.q_ref, bf16[4096,128]{1,0:T(8,128)(2,1)S(1)} %get-tuple-element.24.k_ref, ...), custom_call_target="tpu_custom_call" | custom-call | tf_op jit(solution)/shard_map/attention_backward/pallas_call | solution.py:325
  78.2 0.0 copy-done
  78.2 0.0 copy-done.1
  78.2 0.0 copy-done.4
  78.2 0.0 copy-done.5
  78.2 54.4 %return_heads.1 = (bf16[128,4096]{1,0:T(8,128)(2,1)S(1)}, bf16[128,4096]{1,0:T(8,128)(2,1)S(1)}, bf16[128,4096]{1,0:T(8,128)(2,1)S(1)}, f32[18,8,128]{2,1,0:T(8,128)S(1)}) custom-call(bf16[4096,128]{1,0:T(8,128)(2,1)S(1)} %get-tuple-element.30.dq_ref, bf16[4096,128]{1,0:T(8,128)(2,1)S(1)} %get-tuple-element.31.dk_ref, ...), custom_call_target="tpu_custom_call" | custom-call | tf_op jit(solution)/shard_map/return_heads/pallas_call | solution.py:570
  132.6 2.3 %write_results.1 = (bf16[128,4096]{1,0:T(8,128)(2,1)}, bf16[128,4096]{1,0:T(8,128)(2,1)}, bf16[128,4096]{1,0:T(8,128)(2,1)}, f32[8,640]{1,0:T(8,128)}, f32[8,512...) custom-call(bf16[128,4096]{1,0:T(8,128)(2,1)S(1)} %get-tuple-element.35.gq, ...), custom_call_target="tpu_custom_call" | custom-call | tf_op jit(solution)/shard_map/write_results/pallas_call | solution.py:626
Async XLA Ops:
  0.6 0.9 copy-start.2
  1.5 0.9 copy-start.3
  2.4 0.7 copy-start.6
  60.4 17.8 %copy-start = (bf16[128,5120]{1,0:T(8,128)(2,1)S(1)}, bf16[128,5120]{1,0:T(8,128)(2,1)}, u32[]{:S(2)}) copy-start(bf16[128,5120]{1,0:T(8,128)(2,1)} %hid.1) | copy-start | bytes 3932164
  60.4 17.8 %copy-start.1 = (f32[4096,128]{1,0:T(8,128)S(1)}, f32[4096,128]{1,0:T(8,128)}, u32[]{:S(2)}) copy-start(f32[4096,128]{1,0:T(8,128)} %get-tuple-element.33.table) | copy-start | bytes 6291460
  60.4 17.8 %copy-start.4 = (bf16[8,4096]{1,0:T(8,128)(2,1)S(1)}, bf16[8,4096]{1,0:T(8,128)(2,1)}, u32[]{:S(2)}) copy-start(bf16[8,4096]{1,0:T(8,128)(2,1)} %upq.1) | copy-start | bytes 196612
  60.5 17.8 %copy-start.5 = (bf16[8,4096]{1,0:T(8,128)(2,1)S(1)}, bf16[8,4096]{1,0:T(8,128)(2,1)}, u32[]{:S(2)}) copy-start(bf16[8,4096]{1,0:T(8,128)(2,1)} %upv.1) | copy-start | bytes 196612
